TPU v7x, 32 devices: a whole 2x2x4 slice. The times are simulated.
32 devices in a mesh: group: 2 (over x), module: 16 (over z, y, core).
Axes of the slice: x: 2, y: 2, z: 4, core: 2. Of those that a mesh axis runs over, the one named last changes fastest.
Arguments:
- query_grads: float32 [16, 32, 128, 128], P(None, None, 'module'), may hold values from -0.1875 to 0.1875
- train_grads: float32 [32, 128, 128, 128], P('module', 'group'), parts along dimension 1, may hold values from -0.1875 to 0.1875
- out_basis: float32 [32, 128, 128], P('module'), may hold values from -0.5 to 0.5
- in_basis: float32 [32, 128, 128], P('module'), may hold values from -0.5 to 0.5
- corrections: float32 [32, 128, 128], P('module'), may hold values from 0.01 to 10
- ranks: int32 [16], replicated, may hold values from 32 to 128
- slot_modules: int32 [32], replicated, may hold values from -1 to 15, as said below
Outputs:
- scores: float32 [32, 128], P(None, 'group'), parts along dimension 1
There are 2 independent parts, one for each index of `group`. A program takes and returns all parts, laid end to end along the dimension named above; an argument that names none is the same for every part. Nothing has to cross between parts.
Inputs may be any that keep to these rules, and one draw needn't show every extreme that they name: `slot_modules`: each module number 0 to 15 stands in exactly one entry; all other entries are -1. Owner i holds the 2 entries from i * 2 on, so an owner holds 0 to 2 modules, and some owner holds 2.
All inputs are finite; a program needn't handle non-finite values.
Results may differ from a plain program's by a relative error of at most 0.0003.
Values sent between devices are 32-bit elements; how exact they have to be, the bound alone decides.
No kernel may reach another device: no remote copies, remote signals or barrier semaphores. Data moves between devices by JAX's collectives and lax.ppermute only.
A program may use at most 128 MiB of HBM per device.

v0:
```python
import jax
import jax.numpy as jnp
from jax import lax
from jax.sharding import PartitionSpec as P


def rotate(field, output_eigenbasis, inner_basis):
    inner = jnp.einsum("noi,ib->nob", field, inner_basis, precision=lax.Precision.HIGHEST)
    return jnp.einsum("oa,nob->nab", output_eigenbasis, inner, precision=lax.Precision.HIGHEST)


def blank_rotation(field, output_eigenbasis, inner_basis):
    return jnp.zeros(field.shape, jnp.float32)


def slot_weight(spectrum, keep_rank):
    damping = 0.1 * jnp.mean(spectrum)
    positions = lax.iota(jnp.int32, spectrum.shape[0])
    kept_mask = (positions[:, None] < keep_rank) & (positions[None, :] < keep_rank)
    return jnp.where(kept_mask, 1.0 / (spectrum + damping), jnp.zeros_like(spectrum))


def score_rotated(query_block, rotated_train, output_eigenbasis, inner_basis, spectrum, keep_rank):
    scaled = rotate(query_block, output_eigenbasis, inner_basis) * slot_weight(spectrum, keep_rank)
    return jnp.einsum("qab,eab->qe", scaled, rotated_train, precision=lax.Precision.HIGHEST)


def blank_scores(query_block, second_block, output_eigenbasis, inner_basis, spectrum, keep_rank):
    return jnp.zeros((query_block.shape[0], second_block.shape[0]), jnp.float32)


def body(query_grads, train_grads, out_basis, in_basis, corrections, ranks, slot_modules):
    slot_count = out_basis.shape[0]
    peer_count = lax.axis_size("module")
    own_index = lax.axis_index("module")
    owned_modules = lax.dynamic_slice_in_dim(slot_modules, own_index * slot_count, slot_count)
    query_count = query_grads.shape[1]
    example_count = train_grads.shape[1]
    rotated = []
    for number in range(slot_count):
        rotated.append(
            lax.cond(
                owned_modules[number] >= 0,
                rotate,
                blank_rotation,
                train_grads[number],
                out_basis[number],
                in_basis[number],
            )
        )
    safe_index = jnp.maximum(slot_modules, 0)
    populated_slots = slot_modules >= 0
    outgoing = jnp.where(populated_slots[:, None, None, None], query_grads[safe_index], 0.0)
    outgoing = outgoing.reshape((peer_count, slot_count) + outgoing.shape[1:])
    received = lax.all_to_all(outgoing, "module", split_axis=0, concat_axis=3, tiled=True)[0]
    running = jnp.zeros((query_count, example_count), jnp.float32)
    for number in range(slot_count):
        module = owned_modules[number]
        keep_rank = ranks[jnp.maximum(module, 0)]
        term = lax.cond(
            module >= 0,
            score_rotated,
            blank_scores,
            received[number],
            rotated[number],
            out_basis[number],
            in_basis[number],
            corrections[number],
            keep_rank,
        )
        running = running + term
    return lax.psum(running, "module")


def solution(mesh):
    return jax.shard_map(
        body,
        mesh=mesh,
        in_specs=(
            P(None, None, "module", None),
            P("module", "group", None, None),
            P("module", None, None),
            P("module", None, None),
            P("module", None, None),
            P(),
            P(),
        ),
        out_specs=P(None, "group"),
        check_vma=False,
    )
```

profile of v0, /device:TPU:0, one launch (start us, length us, event | category | flops | bytes accessed | tf_op | source)
XLA Modules:
  0.0 223.0 jit_solution(18283808478415897497)
XLA Ops:
  0.0 0.0 copy-start
  0.0 0.8 broadcast_maximum_fusion
  0.8 0.7 broadcast_compare_fusion
  1.5 0.1 broadcast_in_dim.24
  1.6 0.0 copy-done
  1.6 2.8 %gather_fusion = f32[32,32,8,128]{3,2,1,0:T(8,128)} fusion(f32[16,32,8,128]{3,2,1,0:T(8,128)S(1)} %copy-done, s32[1024]{0:T(1024)S(1)} %pad_clamp_fusion), kind=kCustom, calls=%fused_computation | custom fusion | bytes 8388736 | tf_op jit(solution)/shard_map/gather | solution.py:53
  4.4 4.8 %broadcast_select_fusion = f32[16,2,32,8,128]{4,3,2,1,0:T(8,128)} fusion(f32[16,2,32,8,128]{4,3,2,1,0:T(8,128)} %bitcast.80, pred[16,2]{1,0:T(8,128)(4,1)S(1)} %broadcast_in_dim.24), kind=kLoop, calls=%fused_computation.37 | loop fusion | flops 1048576 | bytes 8388640 | tf_op jit(solution)/shard_map/jit(_where)/select_n | solution.py:53
  9.1 0.0 copy-start.4
  9.1 0.0 copy-start.2
  9.1 0.0 copy-start.3
  9.1 7.6 %all-to-all-start = ((f32[16,2,32,8,128]{4,3,2,1,0:T(8,128)}), f32[16,2,32,8,128]{4,3,2,1,0:T(8,128)}, u32[]{:S(2)}, u32[]{:S(2)}) async-start(f32[16,2,32,8,128]{4,3,2,1,0:T(8,128)} %broadcast_select_fusion), calls=%async_computation | async-start | bytes 8388608 | tf_op jit(solution)/shard_map/all_to_all | solution.py:55
  16.7 0.0 copy-done.4
  16.7 0.1 dynamic_slice.11
  16.8 0.6 fusion.24
  18.7 0.0 copy-done.2
  18.8 0.0 copy-done.3
  18.8 2.5 %conditional.6 = (f32[64,128,128]{1,2,0:T(8,128)}) conditional(s32[]{:T(128)} %convert_element_type.9, () %tuple.34, (f32[2,64,128,128]{3,2,1,0:T(8,128)}, f32[128,128]{1,0:T(8,128)S(1)}, f32[128,128]{1,0:T(8,128)S(1)}) %tuple.35), branch_computations={%region_5.6_spmd, %region_6.0_spmd} | conditional | flops 3221225472 | bytes 16908296 | solution.py:42
  18.8 2.4 %broadcast.55 = f32[64,128,128]{1,2,0:T(8,128)} broadcast(f32[]{:T(128)} %constant.18.clone), dimensions={} | broadcast | bytes 4194308 | tf_op jit(solution)/shard_map/broadcast.4
  21.2 0.0 copy-start.1
  21.2 0.0 copy-start.5
  21.3 2.5 %conditional.4 = (f32[64,128,128]{1,2,0:T(8,128)}) conditional(s32[]{:T(128)} %convert_element_type.8, () %tuple.30, (f32[2,64,128,128]{3,2,1,0:T(8,128)}, f32[128,128]{1,0:T(8,128)S(1)}, f32[128,128]{1,0:T(8,128)S(1)}) %tuple.31), branch_computations={%region_0.0_spmd, %region_1.0_spmd} | conditional | flops 3221225472 | bytes 16908296 | solution.py:42
  21.3 2.5 %broadcast.51 = f32[64,128,128]{1,2,0:T(8,128)} broadcast(f32[]{:T(128)} %constant.8.clone), dimensions={} | broadcast | bytes 4194308 | tf_op jit(solution)/shard_map/broadcast.2
  23.7 70.5 %all-to-all-done = f32[16,2,32,8,128]{4,3,2,1,0:T(8,128)} async-done(((f32[16,2,32,8,128]{4,3,2,1,0:T(8,128)}), f32[16,2,32,8,128]{4,3,2,1,0:T(8,128)}, u32[]{:S(2)}, u32[]{:S(2)}) %all-to-all-start) | async-done | bytes 4194336 | tf_op jit(solution)/shard_map/all_to_all | solution.py:55
  94.3 0.0 copy-done.1
  94.3 0.0 copy-done.5
  94.3 0.2 conditional.7
  94.5 0.2 conditional.5
  94.7 128.2 %psum.7 = f32[32,64]{1,0:T(8,128)} all-reduce(f32[32,64]{1,0:T(8,128)S(1)} %add.27), channel_id=1, replica_groups=mesh['group'=2,'module'=16] {'module'}, use_global_device_ids=true, to_apply=%region_10.11 | all-reduce | flops 2048 | bytes 16384 | tf_op jit(solution)/shard_map/psum | solution.py:72
  (5 shorter events, 0.0 us)
Async XLA Ops:
  0.0 1.6 copy-start
  9.1 7.6 %copy-start.4 = (s32[32]{0:T(128)S(1)}, s32[32]{0:T(128)}, u32[]{:S(2)}) copy-start(s32[32]{0:T(128)} %param.21) | copy-start | bytes 388
  9.1 9.6 %copy-start.2 = (f32[2,128,128]{2,1,0:T(8,128)S(1)}, f32[2,128,128]{2,1,0:T(8,128)}, u32[]{:S(2)}) copy-start(f32[2,128,128]{2,1,0:T(8,128)} %param.17) | copy-start | bytes 393220
  9.1 9.6 %copy-start.3 = (f32[2,128,128]{2,1,0:T(8,128)S(1)}, f32[2,128,128]{2,1,0:T(8,128)}, u32[]{:S(2)}) copy-start(f32[2,128,128]{2,1,0:T(8,128)} %param.18) | copy-start | bytes 393220
  9.1 85.1 %all-to-all-start = ((f32[16,2,32,8,128]{4,3,2,1,0:T(8,128)}), f32[16,2,32,8,128]{4,3,2,1,0:T(8,128)}, u32[]{:S(2)}, u32[]{:S(2)}) async-start(f32[16,2,32,8,128]{4,3,2,1,0:T(8,128)} %broadcast_select_fusion), calls=%async_computation | async-start | bytes 8388608 | tf_op jit(solution)/shard_map/all_to_all | solution.py:55
  21.2 73.0 %copy-start.1 = (f32[2,128,128]{2,1,0:T(8,128)S(1)}, f32[2,128,128]{2,1,0:T(8,128)}, u32[]{:S(2)}) copy-start(f32[2,128,128]{2,1,0:T(8,128)} %param.19) | copy-start | bytes 393220
  21.2 73.0 %copy-start.5 = (s32[16]{0:T(128)S(1)}, s32[16]{0:T(128)}, u32[]{:S(2)}) copy-start(s32[16]{0:T(128)} %param.20) | copy-start | bytes 196
where the time goes:
time: 224 us; the launch traced here: 223 us
  blocking collectives  128 us (57%)
  waiting for transfers between devices  70.5 us (31%)
  local copies, waits for them, and re-layouts  8.53 us (4%)
  starting transfers between devices  7.6 us (3%)
  other arithmetic  6.23 us (3%)
    psum x1, blocking collectives, body(): return lax.psum(running, 'module')  128 us
    all_to_all x1, waiting for transfers between devices, body(): lax.all_to_all(outgoing, 'module', split_axis=0, concat_axis=3, tiled=True)  70.5 us
    all_to_all x1, starting transfers between devices, body(): lax.all_to_all(outgoing, 'module', split_axis=0, concat_axis=3, tiled=True)  7.6 us
    another operation x4, local copies, waits for them, and re-layouts  4.93 us
    select_n x1, other arithmetic, body(): jnp.where(populated_slots[:, None, None, None], query_grads[safe_index],...  4.75 us
  transfers between devices with their start and end apart: 1, of which 1 were waited for; matrix products, arithmetic and copies ran while one was open for 3% of the time, Pallas kernels for 0%

commit v1 on v0

v1 whole, which is shorter than its diff:
```python
import functools
import jax
import jax.numpy as jnp
from jax import lax
from jax.experimental import pallas as pl
from jax.experimental.pallas import tpu as pltpu
from jax.sharding import PartitionSpec as P

F32 = jnp.float32
BF16 = jnp.bfloat16
NT = (((1,), (1,)), ((), ()))
NN = (((1,), (0,)), ((), ()))


def entry_slot(slots, owner, core, entry):
    probe = slots[2 * owner + core]
    return jnp.where(probe < 0, 1 - entry, entry)


def chip_list(slots, chip, cap):
    found = []
    for core in range(2):
        owner = chip * 2 + core
        found.append([slots[2 * owner + entry_slot(slots, owner, core, e)] for e in range(2)])
    if cap == 4:
        return found[0] + found[1]
    return [found[0][0], jnp.maximum(found[0][1], found[1][0]), found[1][1]]


def split(x):
    high = x.astype(BF16)
    return high, (x - high.astype(F32)).astype(BF16)


def pack_kernel(chips, cap, share, slots, place, query, own, *sends):
    chip, group = place[0], place[2]
    rows = query.shape[2]
    for k, module in enumerate(chip_list(slots, chip, cap)):
        module = jnp.maximum(module, 0)
        for r in range(rows):
            own[k, r] = query[module, :, r, :]
    start = pl.multiple_of(group * share, share)
    for d in range(1, chips):
        for k, module in enumerate(chip_list(slots, chip ^ d, cap)):
            module = jnp.maximum(module, 0)
            for r in range(rows):
                sends[d - 1][k, r] = query[module, pl.ds(start, share), r, :]


def pack(chips, cap, share, slots, place, query):
    _, count, rows, width = query.shape
    vmem = pl.BlockSpec(memory_space=pltpu.VMEM)
    return pl.pallas_call(
        functools.partial(pack_kernel, chips, cap, share),
        grid_spec=pltpu.PrefetchScalarGridSpec(
            num_scalar_prefetch=2,
            grid=(),
            in_specs=[vmem],
            out_specs=[vmem] * chips,
        ),
        out_shape=[jax.ShapeDtypeStruct((cap, rows, count, width), F32)]
        + [jax.ShapeDtypeStruct((cap, rows, share, width), F32)] * (chips - 1),
        cost_estimate=pl.CostEstimate(flops=0, bytes_accessed=2 * query.size * 4, transcendentals=0),
        name="pack",
    )(slots, place, query)


def fold_kernel(chips, slots, place, ranks, train, out_basis, in_basis, corrections, mine, other,
                w_in, w_out, w_out_t, w_in_t, weight, turned):
    core = place[1]
    owner = place[0] * 2 + core
    entry = pl.program_id(0)
    block, dim = train.shape[1], train.shape[2]
    rows = dim // (2 * chips)

    @pl.when(pl.program_id(1) == 0)
    def _():
        module = slots[2 * owner + entry_slot(slots, owner, core, entry)]
        rank = jnp.where(module >= 0, ranks[jnp.maximum(module, 0)], 0)
        spectrum = corrections[0]
        damping = 0.1 * (jnp.sum(spectrum) / (dim * dim))
        a = lax.broadcasted_iota(jnp.int32, (dim, dim), 0)
        b = lax.broadcasted_iota(jnp.int32, (dim, dim), 1)
        kept = jnp.where((a < rank) & (b < rank), 1.0 / (spectrum + damping), 0.0)
        weight[...] = kept.T
        for ref, value in ((w_in, in_basis[0]), (w_out, out_basis[0]),
                           (w_out_t, out_basis[0].T), (w_in_t, in_basis[0].T)):
            high, low = split(value)
            both = jnp.concatenate([high, low], axis=1)
            ref[...] = jnp.concatenate([both, both], axis=0)

    def times(x, ref):
        flat = x.reshape(block * dim, dim)
        high, low = split(flat)
        product = lax.dot_general(jnp.concatenate([high, low], axis=1), ref[...], NN, preferred_element_type=F32)
        return (product[:, :dim] + product[:, dim:]).reshape(block, dim, dim)

    x = times(train[0], w_in)
    x = times(jnp.swapaxes(x, 1, 2), w_out) * weight[...][None]
    x = jnp.swapaxes(times(x, w_out_t), 1, 2)
    turned[...] = times(x, w_in_t).reshape(block * dim, dim)
    for chip in range(chips):
        for r in range(rows):
            here = (chip * 2 + core) * rows + r
            there = (chip * 2 + 1 - core) * rows + r
            mine[0, chip, r] = turned[pl.ds(here, block, stride=dim), :]
            other[0, chip, r] = turned[pl.ds(there, block, stride=dim), :]


def fold(chips, part, parts, slots, place, ranks, train, out_basis, in_basis, corrections):
    entries, examples, dim, _ = train.shape
    rows = dim // (2 * chips)
    block = 8
    size = examples // parts
    steps = size // block

    def slot_of(entry, slots, place):
        return entry_slot(slots, place[0] * 2 + place[1], place[1], entry)

    square = pl.BlockSpec((1, dim, dim), lambda n, b, s, p, r: (slot_of(n, s, p), 0, 0))
    out = pl.BlockSpec((1, chips, rows, block, dim), lambda n, b, s, p, r: (n, 0, 0, b, 0))
    shape = jax.ShapeDtypeStruct((entries, chips, rows, size, dim), F32)
    double = pltpu.VMEM((2 * dim, 2 * dim), BF16)
    return pl.pallas_call(
        functools.partial(fold_kernel, chips),
        grid_spec=pltpu.PrefetchScalarGridSpec(
            num_scalar_prefetch=3,
            grid=(entries, steps),
            in_specs=[pl.BlockSpec((1, block, dim, dim), lambda n, b, s, p, r: (slot_of(n, s, p), part * steps + b, 0, 0)),
                      square, square, square],
            out_specs=[out, out],
            scratch_shapes=[double] * 4 + [pltpu.VMEM((dim, dim), F32), pltpu.VMEM((block * dim, dim), F32)],
        ),
        out_shape=[shape, shape],
        compiler_params=pltpu.CompilerParams(vmem_limit_bytes=48 << 20),
        cost_estimate=pl.CostEstimate(flops=entries * size * 8 * dim**3 * 4, bytes_accessed=entries * size * dim * dim * 8, transcendentals=0),
        name="fold",
    )(slots, place, ranks, train, out_basis, in_basis, corrections)


def score_kernel(cap, shifts, groups, share, parts, place, *refs):
    core, group = place[1], place[2]
    refs = list(refs)
    previous, out = refs.pop(0), refs.pop()
    total = None
    for d in shifts:
        if d == 0:
            own = refs.pop(0)
            queries = [own.at[:, :, pl.ds(pl.multiple_of((group ^ t) * share, share), share), :] for t in range(groups)]
        else:
            queries = [refs.pop(0) for _ in range(groups)]
        folded = [[refs.pop(0) for _ in range(parts)] for _ in range(2)]
        rows = folded[0][0].shape[2]
        for side in range(2):
            for entry in range(2):
                position = jnp.where(core == side, 0, cap - 2) + entry
                high, low = split(jnp.concatenate(
                    [jnp.concatenate([q[position, r] for q in queries], axis=0) for r in range(rows)], axis=1))
                left = jnp.concatenate([high, low], axis=0)
                high, low = split(jnp.concatenate(
                    [jnp.concatenate([g[entry, 0, r] for g in folded[side]], axis=0) for r in range(rows)], axis=1))
                right = jnp.concatenate([high, low], axis=0)
                product = lax.dot_general(left, right, NT, preferred_element_type=F32)
                total = product if total is None else total + product
    half, examples = total.shape[0] // 2, total.shape[1] // 2
    result = (total[:half, :examples] + total[half:, examples:]) + (total[:half, examples:] + total[half:, :examples])
    out[...] = result + previous[...]


def score(cap, shifts, groups, share, place, previous, queries, folded):
    parts = len(folded[0])
    vmem = pl.BlockSpec(memory_space=pltpu.VMEM)
    operands, specs = [previous], [vmem]
    for d, query in zip(shifts, queries):
        operands += query
        specs += [vmem] * len(query)
        for side in folded:
            for g in side:
                operands.append(g)
                specs.append(pl.BlockSpec((g.shape[0], 1) + g.shape[2:], lambda n, p, d=d: (0, p[0] ^ d, 0, 0, 0)))
    return pl.pallas_call(
        functools.partial(score_kernel, cap, shifts, groups, share, parts),
        grid_spec=pltpu.PrefetchScalarGridSpec(
            num_scalar_prefetch=1, grid=(1,), in_specs=specs, out_specs=vmem),
        out_shape=jax.ShapeDtypeStruct(previous.shape, F32),
        compiler_params=pltpu.CompilerParams(vmem_limit_bytes=48 << 20),
        cost_estimate=pl.CostEstimate(flops=len(shifts) * 4 * 2 * 64 * 128 * 1024, bytes_accessed=len(shifts) * 1536 * 1024, transcendentals=0),
        name="score",
    )(place, *operands)


def order_of(chips):
    return sorted(range(1, chips), key=lambda d: (d.bit_length() > 2, -d if d.bit_length() > 2 else d))


def body(devices, groups, query_grads, train_grads, out_basis, in_basis, corrections, ranks, slot_modules):
    chips, cap, parts = devices // 2, 4, 4
    count, examples = query_grads.shape[1], train_grads.shape[1]
    share = count // groups
    index, group = lax.axis_index("module"), lax.axis_index("group")
    place = jnp.stack([index // 2, index % 2, group]).astype(jnp.int32)
    own, *sends = pack(chips, cap, share, slot_modules, place, query_grads)
    order = order_of(chips)
    arrived = {0: [own]}
    for d in order:
        direct = lax.ppermute(sends[d - 1], "module", [(i, i ^ (2 * d)) for i in range(devices)])
        arrived[d] = [direct]
        for t in range(1, groups):
            arrived[d].append(lax.ppermute(direct, "group", [(i, i ^ t) for i in range(groups)]))
    mine, other = [], []
    for part in range(parts):
        here, there = fold(chips, part, parts, slot_modules, place, ranks, train_grads, out_basis, in_basis, corrections)
        mine.append(here)
        other.append(lax.ppermute(there, "module", [(i, i ^ 1) for i in range(devices)]))
    total = jnp.zeros((count, examples), F32)
    everything = [0] + order
    step = max(len(everything) // 4, 1)
    for first in range(0, len(everything), step):
        shifts = tuple(everything[first:first + step])
        total = score(cap, shifts, groups, share, place, total, [arrived[d] for d in shifts], [mine, other])
    blocks = total.reshape(groups, share, examples)
    total = blocks[jnp.arange(groups) ^ group].reshape(count, examples)
    stride = 1
    while stride < devices:
        total = total + lax.ppermute(total, "module", [(i, i ^ stride) for i in range(devices)])
        stride *= 2
    return total


def solution(mesh):
    devices, groups = mesh.shape["module"], mesh.shape["group"]

    def whole(*arrays):
        return body(devices, groups, *arrays)

    return jax.shard_map(
        whole,
        mesh=mesh,
        in_specs=(
            P(None, None, "module", None),
            P("module", "group", None, None),
            P("module", None, None),
            P("module", None, None),
            P("module", None, None),
            P(),
            P(),
        ),
        out_specs=P(None, "group"),
        check_vma=False,
    )
```

time: 224 us -> 135 us (0.60)
  blocking collectives: 128 us -> 0 us
  Pallas kernels: 0 us -> 46 us
  starting transfers between devices: 7.6 us -> 20.9 us
  waiting for transfers between devices: 70.5 us -> 59.3 us
  other arithmetic: 6.23 us -> 1.31 us
    psum x1 -> x0, blocking collectives: 128 us -> none  [body(): return lax.psum(running, 'module')]
    all_to_all x1 -> x0, waiting for transfers between devices: 70.5 us -> none  [body(): lax.all_to_all(outgoing, 'module', split_axis=0, concat_axis=3, tiled=True)]
    ppermute x0 -> x22, waiting for transfers between devices: none -> 59.3 us  [the longest x7 26.3 us: body(): lax.ppermute(direct, 'group', [(i, i ^ t) for i in range(groups)])]
    pallas_call x0 -> x9, Pallas kernels: none -> 46 us  [the longest x4 29.5 us: fold(): pl.pallas_call(functools.partial(fold_kernel, chips), grid_spec=pltpu.Pre...]
    ppermute x0 -> x22, starting transfers between devices: none -> 20.9 us  [the longest x7 10.5 us: body(): lax.ppermute(sends[d - 1], 'module', [(i, i ^ 2 * d) for i in range(devic...]
    all_to_all x1 -> x0, starting transfers between devices: 7.6 us -> none  [body(): lax.all_to_all(outgoing, 'module', split_axis=0, concat_axis=3, tiled=True)]
    unnamed x12 -> x28, local copies, waits for them, and re-layouts: 0.06 us -> 6.17 us
    another operation x4 -> x0, local copies, waits for them, and re-layouts: 4.93 us -> none
  transfers between devices with their start and end apart: 1 -> 22, of which waited for: 1 -> 12; matrix products, arithmetic and copies ran while one was open for 3% -> 0% of each run, Pallas kernels for 0% -> 28%
where the time goes in v1:
time: 135 us; the launch traced here: 134 us
  waiting for transfers between devices  59.3 us (44%)
  Pallas kernels  46 us (34%)
  starting transfers between devices  20.9 us (15%)
  local copies, waits for them, and re-layouts  6.73 us (5%)
    pallas_call x4, Pallas kernels, fold(): pl.pallas_call(functools.partial(fold_kernel, chips), grid_spec=pltpu.Pre...  29.5 us
    ppermute x7, waiting for transfers between devices, body(): lax.ppermute(direct, 'group', [(i, i ^ t) for i in range(groups)])  26.3 us
    ppermute x7, waiting for transfers between devices, body(): lax.ppermute(sends[d - 1], 'module', [(i, i ^ 2 * d) for i in range(devic...  20.8 us
    ppermute x4, waiting for transfers between devices, body(): lax.ppermute(total, 'module', [(i, i ^ stride) for i in range(devices)])  12.2 us
    pallas_call x4, Pallas kernels, score(): pl.pallas_call(functools.partial(score_kernel, cap, shifts, groups, share...  11.6 us
    ppermute x7, starting transfers between devices, body(): lax.ppermute(sends[d - 1], 'module', [(i, i ^ 2 * d) for i in range(devic...  10.5 us
    ppermute x7, starting transfers between devices, body(): lax.ppermute(direct, 'group', [(i, i ^ t) for i in range(groups)])  8.1 us
    unnamed x28, local copies, waits for them, and re-layouts  6.17 us
  transfers between devices with their start and end apart: 22, of which 12 were waited for; matrix products, arithmetic and copies ran while one was open for 0% of the time, Pallas kernels for 28%

profile of v1, /device:TPU:0, one launch (start us, length us, event | category | flops | bytes accessed | tf_op | source)
XLA Modules:
  0.0 134.4 jit_solution(1530707156433027254)
XLA Ops:
  0.0 0.7 pad_add_fusion.place
  0.7 5.0 %pack.1 = (f32[4,8,32,128]{3,2,1,0:T(8,128)}, f32[4,8,16,128]{3,2,1,0:T(8,128)}, f32[4,8,16,128]{3,2,1,0:T(8,128)}, f32[4,8,16,128]{3,2,1,0:T(8,128)}, f32[4,8,1...) custom-call(s32[32]{0:T(128)} %slots.9, ...), custom_call_target="tpu_custom_call" | custom-call | bytes 4194304 | tf_op jit(solution)/shard_map/pack/pallas_call | solution.py:53
  5.6 3.0 %collective-permute-start.4 = (f32[4,8,16,128]{3,2,1,0:T(8,128)}, f32[4,8,16,128]{3,2,1,0:T(8,128)S(1)}, u32[]{:S(2)}, u32[]{:S(2)}) collective-permute-start(f32[4,8,16,128]{3,2,1,0:T(8,128)} %get-tuple-element.30), channel_id=1, source_target_pairs={{0,2},{1,3},{2,0},{3,1},{4,6},{5,7},{6,4},{7,5},{8,10},{9,11},{10,... | collective-permute-start | bytes 786440 | tf_op jit(solution)/shard_map/ppermute | solution.py:206
  8.6 1.6 %collective-permute-start.6 = (f32[4,8,16,128]{3,2,1,0:T(8,128)}, f32[4,8,16,128]{3,2,1,0:T(8,128)S(1)}, u32[]{:S(2)}, u32[]{:S(2)}) collective-permute-start(f32[4,8,16,128]{3,2,1,0:T(8,128)} %get-tuple-element.31), channel_id=1, source_target_pairs={{0,4},{1,5},{2,6},{3,7},{4,0},{5,1},{6,2},{7,3},{8,12},{9,13},{10,... | collective-permute-start | bytes 786440 | tf_op jit(solution)/shard_map/ppermute | solution.py:206
  10.2 4.9 %collective-permute-start.10 = (f32[4,8,16,128]{3,2,1,0:T(8,128)}, f32[4,8,16,128]{3,2,1,0:T(8,128)S(1)}, u32[]{:S(2)}, u32[]{:S(2)}) collective-permute-start(f32[4,8,16,128]{3,2,1,0:T(8,128)} %get-tuple-element.33), channel_id=1, source_target_pairs={{0,14},{1,15},{2,12},{3,13},{4,10},{5,11},{6,8},{7,9},{8,6},{9,7},... | collective-permute-start | bytes 786440 | tf_op jit(solution)/shard_map/ppermute | solution.py:206
  15.1 0.2 collective-permute-start.12
  15.4 0.9 copy-done
  16.3 0.9 copy-done.1
  17.2 0.9 copy-done.2
  18.1 0.7 copy-done.4
  18.8 0.7 copy-done.6
  19.4 0.7 copy-done.7
  20.1 7.4 %fold.4 = (f32[2,8,8,16,128]{4,3,2,1,0:T(8,128)S(1)}, f32[2,8,8,16,128]{4,3,2,1,0:T(8,128)S(1)}) custom-call(s32[32]{0:T(128)S(1)} %copy-done.6, s32[3]{0:T(128)S(1)} %copy-done.4, s32[16]{0:T(128)S(1)} %copy-done.7, f32[2,64,128,128]{3,2,1,0:T(8,128)} %train.7, f32[2,128,128]{2,1,0:T(8,128)S(1)} %copy-done, f32[2,128,128]{2,1,0:T(8,128)S(1)} %copy-done.1, ...), custom_call_target="tpu_custom_call" | custom-call | flops 2147483648 | bytes 4194304 | tf_op jit(solution)/shard_map/fold/pallas_call | solution.py:124
  27.5 7.4 %fold.5 = (f32[2,8,8,16,128]{4,3,2,1,0:T(8,128)S(1)}, f32[2,8,8,16,128]{4,3,2,1,0:T(8,128)S(1)}) custom-call(s32[32]{0:T(128)S(1)} %copy-done.6, s32[3]{0:T(128)S(1)} %copy-done.4, s32[16]{0:T(128)S(1)} %copy-done.7, f32[2,64,128,128]{3,2,1,0:T(8,128)} %train.7, f32[2,128,128]{2,1,0:T(8,128)S(1)} %copy-done, f32[2,128,128]{2,1,0:T(8,128)S(1)} %copy-done.1, ...), custom_call_target="tpu_custom_call" | custom-call | flops 2147483648 | bytes 4194304 | tf_op jit(solution)/shard_map/fold/pallas_call | solution.py:124
  34.9 7.4 %fold.6 = (f32[2,8,8,16,128]{4,3,2,1,0:T(8,128)S(1)}, f32[2,8,8,16,128]{4,3,2,1,0:T(8,128)S(1)}) custom-call(s32[32]{0:T(128)S(1)} %copy-done.6, s32[3]{0:T(128)S(1)} %copy-done.4, s32[16]{0:T(128)S(1)} %copy-done.7, f32[2,64,128,128]{3,2,1,0:T(8,128)} %train.7, f32[2,128,128]{2,1,0:T(8,128)S(1)} %copy-done, f32[2,128,128]{2,1,0:T(8,128)S(1)} %copy-done.1, ...), custom_call_target="tpu_custom_call" | custom-call | flops 2147483648 | bytes 4194304 | tf_op jit(solution)/shard_map/fold/pallas_call | solution.py:124
  42.4 0.5 collective-permute-start.1
  42.9 0.7 collective-permute-start.14
  43.6 7.4 %fold.7 = (f32[2,8,8,16,128]{4,3,2,1,0:T(8,128)S(1)}, f32[2,8,8,16,128]{4,3,2,1,0:T(8,128)S(1)}) custom-call(s32[32]{0:T(128)S(1)} %copy-done.6, s32[3]{0:T(128)S(1)} %copy-done.4, s32[16]{0:T(128)S(1)} %copy-done.7, f32[2,64,128,128]{3,2,1,0:T(8,128)} %train.7, f32[2,128,128]{2,1,0:T(8,128)S(1)} %copy-done, f32[2,128,128]{2,1,0:T(8,128)S(1)} %copy-done.1, ...), custom_call_target="tpu_custom_call" | custom-call | flops 2147483648 | bytes 4194304 | tf_op jit(solution)/shard_map/fold/pallas_call | solution.py:124
  51.1 0.5 collective-permute-start.3
  51.6 7.0 %collective-permute-done.14.refs_1_ = f32[4,8,16,128]{3,2,1,0:T(8,128)S(1)} collective-permute-done((f32[4,8,16,128]{3,2,1,0:T(8,128)S(1)}, f32[4,8,16,128]{3,2,1,0:T(8,128)S(1)}, u32[]{:S(2)}, u32[]{:S(2)}) %collective-permute-start.14) | collective-permute-done | bytes 262176 | tf_op jit(solution)/shard_map/ppermute | solution.py:206
  58.6 13.8 %collective-permute-done.16.refs_11_ = f32[4,8,16,128]{3,2,1,0:T(8,128)S(1)} collective-permute-done((f32[4,8,16,128]{3,2,1,0:T(8,128)S(1)}, f32[4,8,16,128]{3,2,1,0:T(8,128)S(1)}, u32[]{:S(2)}, u32[]{:S(2)}) %collective-permute-start.16) | collective-permute-done | bytes 262176 | tf_op jit(solution)/shard_map/ppermute | solution.py:206
  72.4 1.5 %collective-permute-start.5 = (f32[4,8,16,128]{3,2,1,0:T(8,128)S(1)}, f32[4,8,16,128]{3,2,1,0:T(8,128)S(1)}, u32[]{:S(2)}, u32[]{:S(2)}) collective-permute-start(f32[4,8,16,128]{3,2,1,0:T(8,128)S(1)} %collective-permute-done.4.refs_10_), channel_id=1, source_target_pairs={{0,16},{16,0},{1,17},{17,1},{2,18},{18,2},{3,19},{19,3},{4,20},{20... | collective-permute-start | bytes 786440 | tf_op jit(solution)/shard_map/ppermute | solution.py:209
  73.9 6.7 %collective-permute-done.5.refs_11_ = f32[4,8,16,128]{3,2,1,0:T(8,128)S(1)} collective-permute-done((f32[4,8,16,128]{3,2,1,0:T(8,128)S(1)}, f32[4,8,16,128]{3,2,1,0:T(8,128)S(1)}, u32[]{:S(2)}, u32[]{:S(2)}) %collective-permute-start.5) | collective-permute-done | bytes 262176 | tf_op jit(solution)/shard_map/ppermute | solution.py:209
  80.6 1.5 %collective-permute-start.7 = (f32[4,8,16,128]{3,2,1,0:T(8,128)S(1)}, f32[4,8,16,128]{3,2,1,0:T(8,128)S(1)}, u32[]{:S(2)}, u32[]{:S(2)}) collective-permute-start(f32[4,8,16,128]{3,2,1,0:T(8,128)S(1)} %collective-permute-done.6.refs_1_), channel_id=1, source_target_pairs={{0,16},{16,0},{1,17},{17,1},{2,18},{18,2},{3,19},{19,3},{4,20},{20... | collective-permute-start | bytes 786440 | tf_op jit(solution)/shard_map/ppermute | solution.py:209
  82.1 5.9 %collective-permute-done.7.refs_2_ = f32[4,8,16,128]{3,2,1,0:T(8,128)S(1)} collective-permute-done((f32[4,8,16,128]{3,2,1,0:T(8,128)S(1)}, f32[4,8,16,128]{3,2,1,0:T(8,128)S(1)}, u32[]{:S(2)}, u32[]{:S(2)}) %collective-permute-start.7) | collective-permute-done | bytes 262176 | tf_op jit(solution)/shard_map/ppermute | solution.py:209
  88.0 1.5 %collective-permute-start.9 = (f32[4,8,16,128]{3,2,1,0:T(8,128)S(1)}, f32[4,8,16,128]{3,2,1,0:T(8,128)S(1)}, u32[]{:S(2)}, u32[]{:S(2)}) collective-permute-start(f32[4,8,16,128]{3,2,1,0:T(8,128)S(1)} %collective-permute-done.8.refs_11_), channel_id=1, source_target_pairs={{0,16},{16,0},{1,17},{17,1},{2,18},{18,2},{3,19},{19,3},{4,20},{20... | collective-permute-start | bytes 786440 | tf_op jit(solution)/shard_map/ppermute | solution.py:209
  89.5 0.5 collective-permute-start.11
  90.0 1.5 %collective-permute-start.13 = (f32[4,8,16,128]{3,2,1,0:T(8,128)S(1)}, f32[4,8,16,128]{3,2,1,0:T(8,128)S(1)}, u32[]{:S(2)}, u32[]{:S(2)}) collective-permute-start(f32[4,8,16,128]{3,2,1,0:T(8,128)S(1)} %collective-permute-done.12.refs_11_), channel_id=1, source_target_pairs={{0,16},{16,0},{1,17},{17,1},{2,18},{18,2},{3,19},{19,3},{4,20},{20... | collective-permute-start | bytes 786440 | tf_op jit(solution)/shard_map/ppermute | solution.py:209
  91.5 0.5 collective-permute-start.15
  92.1 0.4 copy-done.10
  92.5 1.0 copy-done.11
  93.5 1.1 collective-permute-start.17
  94.6 2.9 %score.4.refs_0_ = f32[32,64]{1,0:T(8,128)S(1)} custom-call(s32[3]{0:T(128)S(1)} %copy-done.5, f32[32,64]{1,0:T(8,128)S(1)} %broadcast_in_dim.4.refs_0_, f32[4,8,32,128]{3,2,1,0:T(8,128)S(1)} %copy-done.3, f32[2,8,8,16,128]{4,3,2,1,0:T(8,128)S(1)} %get-tuple-element.22.refs_2_.refs_12_.refs_3_.refs_13_, ...), custom_call_target="tpu_custom_call" | custom-call | flops 134217728 | bytes 3145728 | tf_op jit(solution)/shard_map/score/pallas_call | solution.py:181
  97.6 2.9 %score.5.refs_0_ = f32[32,64]{1,0:T(8,128)S(1)} custom-call(s32[3]{0:T(128)S(1)} %copy-done.5, f32[32,64]{1,0:T(8,128)S(1)} %score.4.refs_0_, f32[4,8,16,128]{3,2,1,0:T(8,128)S(1)} %collective-permute-done.6.refs_1_, f32[4,8,16,128]{3,2,1,0:T(8,128)S(1)} %collective-permute-done.7.refs_2_, ...), custom_call_target="tpu_custom_call" | custom-call | flops 134217728 | bytes 3145728 | tf_op jit(solution)/shard_map/score/pallas_call | solution.py:181
  100.4 2.3 %collective-permute-done.11.refs_2_ = f32[4,8,16,128]{3,2,1,0:T(8,128)S(1)} collective-permute-done((f32[4,8,16,128]{3,2,1,0:T(8,128)S(1)}, f32[4,8,16,128]{3,2,1,0:T(8,128)S(1)}, u32[]{:S(2)}, u32[]{:S(2)}) %collective-permute-start.11) | collective-permute-done | bytes 262176 | tf_op jit(solution)/shard_map/ppermute | solution.py:209
  102.8 5.6 %collective-permute-done.13.refs_12_ = f32[4,8,16,128]{3,2,1,0:T(8,128)S(1)} collective-permute-done((f32[4,8,16,128]{3,2,1,0:T(8,128)S(1)}, f32[4,8,16,128]{3,2,1,0:T(8,128)S(1)}, u32[]{:S(2)}, u32[]{:S(2)}) %collective-permute-start.13) | collective-permute-done | bytes 262176 | tf_op jit(solution)/shard_map/ppermute | solution.py:209
  108.4 2.9 %score.6.refs_0_ = f32[32,64]{1,0:T(8,128)S(1)} custom-call(s32[3]{0:T(128)S(1)} %copy-done.5, f32[32,64]{1,0:T(8,128)S(1)} %score.5.refs_0_, f32[4,8,16,128]{3,2,1,0:T(8,128)S(1)} %collective-permute-done.10.refs_1_, f32[4,8,16,128]{3,2,1,0:T(8,128)S(1)} %collective-permute-done.11.refs_2_, ...), custom_call_target="tpu_custom_call" | custom-call | flops 134217728 | bytes 3145728 | tf_op jit(solution)/shard_map/score/pallas_call | solution.py:181
  111.3 2.7 %collective-permute-done.15.refs_2_ = f32[4,8,16,128]{3,2,1,0:T(8,128)S(1)} collective-permute-done((f32[4,8,16,128]{3,2,1,0:T(8,128)S(1)}, f32[4,8,16,128]{3,2,1,0:T(8,128)S(1)}, u32[]{:S(2)}, u32[]{:S(2)}) %collective-permute-start.15) | collective-permute-done | bytes 262176 | tf_op jit(solution)/shard_map/ppermute | solution.py:209
  114.0 3.0 %collective-permute-done.17.refs_12_ = f32[4,8,16,128]{3,2,1,0:T(8,128)S(1)} collective-permute-done((f32[4,8,16,128]{3,2,1,0:T(8,128)S(1)}, f32[4,8,16,128]{3,2,1,0:T(8,128)S(1)}, u32[]{:S(2)}, u32[]{:S(2)}) %collective-permute-start.17) | collective-permute-done | bytes 262176 | tf_op jit(solution)/shard_map/ppermute | solution.py:209
  117.0 2.9 %score.7 = f32[32,64]{1,0:T(8,128)S(1)} custom-call(s32[3]{0:T(128)S(1)} %copy-done.5, f32[32,64]{1,0:T(8,128)S(1)} %score.6.refs_0_, f32[4,8,16,128]{3,2,1,0:T(8,128)S(1)} %collective-permute-done.14.refs_1_, f32[4,8,16,128]{3,2,1,0:T(8,128)S(1)} %collective-permute-done.15.refs_2_, ...), custom_call_target="tpu_custom_call" | custom-call | flops 134217728 | bytes 3145728 | tf_op jit(solution)/shard_map/score/pallas_call | solution.py:181
  119.9 0.6 gather_fusion
  120.5 1.2 collective-permute-done.18
  121.7 0.4 collective-permute-start.19
  122.1 3.3 %collective-permute-done.19 = f32[32,64]{1,0:T(8,128)S(1)} collective-permute-done((f32[32,64]{1,0:T(8,128)S(1)}, f32[32,64]{1,0:T(8,128)S(1)}, u32[]{:S(2)}, u32[]{:S(2)}) %collective-permute-start.19) | collective-permute-done | bytes 8224 | tf_op jit(solution)/shard_map/ppermute | solution.py:225
  125.4 3.7 %collective-permute-done.20 = f32[32,64]{1,0:T(8,128)S(1)} collective-permute-done((f32[32,64]{1,0:T(8,128)S(1)}, f32[32,64]{1,0:T(8,128)S(1)}, u32[]{:S(2)}, u32[]{:S(2)}) %collective-permute-start.20) | collective-permute-done | bytes 8224 | tf_op jit(solution)/shard_map/ppermute | solution.py:225
  129.2 0.7 collective-permute-start.21
  129.8 4.0 %collective-permute-done.21 = f32[32,64]{1,0:T(8,128)S(1)} collective-permute-done((f32[32,64]{1,0:T(8,128)S(1)}, f32[32,64]{1,0:T(8,128)S(1)}, u32[]{:S(2)}, u32[]{:S(2)}) %collective-permute-start.21) | collective-permute-done | bytes 8224 | tf_op jit(solution)/shard_map/ppermute | solution.py:225
  133.8 0.6 add.32
  (42 shorter events, 0.3 us)
Async XLA Ops:
  5.6 36.6 %collective-permute-start.4 = (f32[4,8,16,128]{3,2,1,0:T(8,128)}, f32[4,8,16,128]{3,2,1,0:T(8,128)S(1)}, u32[]{:S(2)}, u32[]{:S(2)}) collective-permute-start(f32[4,8,16,128]{3,2,1,0:T(8,128)} %get-tuple-element.30), channel_id=1, source_target_pairs={{0,2},{1,3},{2,0},{3,1},{4,6},{5,7},{6,4},{7,5},{8,10},{9,11},{10,... | collective-permute-start | bytes 786440 | tf_op jit(solution)/shard_map/ppermute | solution.py:206
  8.6 33.7 %collective-permute-start.6 = (f32[4,8,16,128]{3,2,1,0:T(8,128)}, f32[4,8,16,128]{3,2,1,0:T(8,128)S(1)}, u32[]{:S(2)}, u32[]{:S(2)}) collective-permute-start(f32[4,8,16,128]{3,2,1,0:T(8,128)} %get-tuple-element.31), channel_id=1, source_target_pairs={{0,4},{1,5},{2,6},{3,7},{4,0},{5,1},{6,2},{7,3},{8,12},{9,13},{10,... | collective-permute-start | bytes 786440 | tf_op jit(solution)/shard_map/ppermute | solution.py:206
  10.2 32.7 %collective-permute-start.8 = (f32[4,8,16,128]{3,2,1,0:T(8,128)}, f32[4,8,16,128]{3,2,1,0:T(8,128)S(1)}, u32[]{:S(2)}, u32[]{:S(2)}) collective-permute-start(f32[4,8,16,128]{3,2,1,0:T(8,128)} %get-tuple-element.32), channel_id=1, source_target_pairs={{0,6},{1,7},{2,4},{3,5},{4,2},{5,3},{6,0},{7,1},{8,14},{9,15},{10,... | collective-permute-start | bytes 786440 | tf_op jit(solution)/shard_map/ppermute | solution.py:206
  10.2 40.8 %collective-permute-start.10 = (f32[4,8,16,128]{3,2,1,0:T(8,128)}, f32[4,8,16,128]{3,2,1,0:T(8,128)S(1)}, u32[]{:S(2)}, u32[]{:S(2)}) collective-permute-start(f32[4,8,16,128]{3,2,1,0:T(8,128)} %get-tuple-element.33), channel_id=1, source_target_pairs={{0,14},{1,15},{2,12},{3,13},{4,10},{5,11},{6,8},{7,9},{8,6},{9,7},... | collective-permute-start | bytes 786440 | tf_op jit(solution)/shard_map/ppermute | solution.py:206
  15.1 35.9 %collective-permute-start.12 = (f32[4,8,16,128]{3,2,1,0:T(8,128)}, f32[4,8,16,128]{3,2,1,0:T(8,128)S(1)}, u32[]{:S(2)}, u32[]{:S(2)}) collective-permute-start(f32[4,8,16,128]{3,2,1,0:T(8,128)} %get-tuple-element.34), channel_id=1, source_target_pairs={{0,12},{1,13},{2,14},{3,15},{4,8},{5,9},{6,10},{7,11},{8,4},{9,5},... | collective-permute-start | bytes 786440 | tf_op jit(solution)/shard_map/ppermute | solution.py:206
  15.4 0.9 copy-start
  16.3 0.9 copy-start.1
  17.2 0.9 copy-start.2
  18.1 0.7 copy-start.4
  18.8 0.7 copy-start.6
  19.4 0.7 copy-start.7
  27.5 15.4 %copy-start.13 = (f32[4,8,16,128]{3,2,1,0:T(8,128)S(1)}, f32[4,8,16,128]{3,2,1,0:T(8,128)}, u32[]{:S(2)}) copy-start(f32[4,8,16,128]{3,2,1,0:T(8,128)} %get-tuple-element.35) | copy-start | bytes 786436
  34.9 23.7 %copy-start.12 = (f32[4,8,16,128]{3,2,1,0:T(8,128)S(1)}, f32[4,8,16,128]{3,2,1,0:T(8,128)}, u32[]{:S(2)}) copy-start(f32[4,8,16,128]{3,2,1,0:T(8,128)} %get-tuple-element.36) | copy-start | bytes 786436
  34.9 59.8 %copy-start.3 = (f32[4,8,32,128]{3,2,1,0:T(8,128)S(1)}, f32[4,8,32,128]{3,2,1,0:T(8,128)}, u32[]{:S(2)}) copy-start(f32[4,8,32,128]{3,2,1,0:T(8,128)} %get-tuple-element.21.refs_1_) | copy-start | bytes 1572868
  34.9 59.8 %copy-start.5 = (s32[3]{0:T(128)S(1)}, s32[3]{0:T(128)}, u32[]{:S(2)}) copy-start(s32[3]{0:T(128)} %pad_add_fusion.place) | copy-start | bytes 40
  42.3 47.2 %collective-permute-start = (f32[2,8,8,16,128]{4,3,2,1,0:T(8,128)S(1)}, f32[2,8,8,16,128]{4,3,2,1,0:T(8,128)S(1)}, u32[]{:S(2)}, u32[]{:S(2)}) collective-permute-start(f32[2,8,8,16,128]{4,3,2,1,0:T(8,128)S(1)} %get-tuple-element.26), channel_id=1, source_target_pairs={{0,1},{1,0},{2,3},{3,2},{4,5},{5,4},{6,7},{7,6},{8,9},{9,8},{10,11... | collective-permute-start | bytes 3145736 | tf_op jit(solution)/shard_map/ppermute | solution.py:214
  42.4 47.7 %collective-permute-start.1 = (f32[2,8,8,16,128]{4,3,2,1,0:T(8,128)S(1)}, f32[2,8,8,16,128]{4,3,2,1,0:T(8,128)S(1)}, u32[]{:S(2)}, u32[]{:S(2)}) collective-permute-start(f32[2,8,8,16,128]{4,3,2,1,0:T(8,128)S(1)} %get-tuple-element.27), channel_id=1, source_target_pairs={{0,1},{1,0},{2,3},{3,2},{4,5},{5,4},{6,7},{7,6},{8,9},{9,8},{10,11... | collective-permute-start | bytes 3145736 | tf_op jit(solution)/shard_map/ppermute | solution.py:214
  42.9 15.7 %collective-permute-start.14 = (f32[4,8,16,128]{3,2,1,0:T(8,128)S(1)}, f32[4,8,16,128]{3,2,1,0:T(8,128)S(1)}, u32[]{:S(2)}, u32[]{:S(2)}) collective-permute-start(f32[4,8,16,128]{3,2,1,0:T(8,128)S(1)} %copy-done.13), channel_id=1, source_target_pairs={{0,10},{1,11},{2,8},{3,9},{4,14},{5,15},{6,12},{7,13},{8,2},{9,3},... | collective-permute-start | bytes 786440 | tf_op jit(solution)/shard_map/ppermute | solution.py:206
  51.0 40.5 %collective-permute-start.2 = (f32[2,8,8,16,128]{4,3,2,1,0:T(8,128)S(1)}, f32[2,8,8,16,128]{4,3,2,1,0:T(8,128)S(1)}, u32[]{:S(2)}, u32[]{:S(2)}) collective-permute-start(f32[2,8,8,16,128]{4,3,2,1,0:T(8,128)S(1)} %get-tuple-element.28), channel_id=1, source_target_pairs={{0,1},{1,0},{2,3},{3,2},{4,5},{5,4},{6,7},{7,6},{8,9},{9,8},{10,11... | collective-permute-start | bytes 3145736 | tf_op jit(solution)/shard_map/ppermute | solution.py:214
  51.1 41.0 %collective-permute-start.3 = (f32[2,8,8,16,128]{4,3,2,1,0:T(8,128)S(1)}, f32[2,8,8,16,128]{4,3,2,1,0:T(8,128)S(1)}, u32[]{:S(2)}, u32[]{:S(2)}) collective-permute-start(f32[2,8,8,16,128]{4,3,2,1,0:T(8,128)S(1)} %get-tuple-element.29), channel_id=1, source_target_pairs={{0,1},{1,0},{2,3},{3,2},{4,5},{5,4},{6,7},{7,6},{8,9},{9,8},{10,11... | collective-permute-start | bytes 3145736 | tf_op jit(solution)/shard_map/ppermute | solution.py:214
  58.6 13.8 %collective-permute-start.16 = (f32[4,8,16,128]{3,2,1,0:T(8,128)S(1)}, f32[4,8,16,128]{3,2,1,0:T(8,128)S(1)}, u32[]{:S(2)}, u32[]{:S(2)}) collective-permute-start(f32[4,8,16,128]{3,2,1,0:T(8,128)S(1)} %copy-done.12), channel_id=1, source_target_pairs={{0,8},{1,9},{2,10},{3,11},{4,12},{5,13},{6,14},{7,15},{8,0},{9,1},... | collective-permute-start | bytes 786440 | tf_op jit(solution)/shard_map/ppermute | solution.py:206
  72.4 8.2 %collective-permute-start.5 = (f32[4,8,16,128]{3,2,1,0:T(8,128)S(1)}, f32[4,8,16,128]{3,2,1,0:T(8,128)S(1)}, u32[]{:S(2)}, u32[]{:S(2)}) collective-permute-start(f32[4,8,16,128]{3,2,1,0:T(8,128)S(1)} %collective-permute-done.4.refs_10_), channel_id=1, source_target_pairs={{0,16},{16,0},{1,17},{17,1},{2,18},{18,2},{3,19},{19,3},{4,20},{20... | collective-permute-start | bytes 786440 | tf_op jit(solution)/shard_map/ppermute | solution.py:209
  80.6 7.4 %collective-permute-start.7 = (f32[4,8,16,128]{3,2,1,0:T(8,128)S(1)}, f32[4,8,16,128]{3,2,1,0:T(8,128)S(1)}, u32[]{:S(2)}, u32[]{:S(2)}) collective-permute-start(f32[4,8,16,128]{3,2,1,0:T(8,128)S(1)} %collective-permute-done.6.refs_1_), channel_id=1, source_target_pairs={{0,16},{16,0},{1,17},{17,1},{2,18},{18,2},{3,19},{19,3},{4,20},{20... | collective-permute-start | bytes 786440 | tf_op jit(solution)/shard_map/ppermute | solution.py:209
  88.0 9.5 %collective-permute-start.9 = (f32[4,8,16,128]{3,2,1,0:T(8,128)S(1)}, f32[4,8,16,128]{3,2,1,0:T(8,128)S(1)}, u32[]{:S(2)}, u32[]{:S(2)}) collective-permute-start(f32[4,8,16,128]{3,2,1,0:T(8,128)S(1)} %collective-permute-done.8.refs_11_), channel_id=1, source_target_pairs={{0,16},{16,0},{1,17},{17,1},{2,18},{18,2},{3,19},{19,3},{4,20},{20... | collective-permute-start | bytes 786440 | tf_op jit(solution)/shard_map/ppermute | solution.py:209
  89.5 5.1 %copy-start.8 = (f32[2,8,8,16,128]{4,3,2,1,0:T(8,128)}, f32[2,8,8,16,128]{4,3,2,1,0:T(8,128)S(1)}, u32[]{:S(2)}) copy-start(f32[2,8,8,16,128]{4,3,2,1,0:T(8,128)S(1)} %collective-permute-done.refs_6_.refs_16_.refs_7_.refs_17_) | copy-start | bytes 3145732
  89.5 13.3 %collective-permute-start.11 = (f32[4,8,16,128]{3,2,1,0:T(8,128)S(1)}, f32[4,8,16,128]{3,2,1,0:T(8,128)S(1)}, u32[]{:S(2)}, u32[]{:S(2)}) collective-permute-start(f32[4,8,16,128]{3,2,1,0:T(8,128)S(1)} %collective-permute-done.10.refs_1_), channel_id=1, source_target_pairs={{0,16},{16,0},{1,17},{17,1},{2,18},{18,2},{3,19},{19,3},{4,20},{20... | collective-permute-start | bytes 786440 | tf_op jit(solution)/shard_map/ppermute | solution.py:209
  90.0 4.6 %copy-start.9 = (f32[2,8,8,16,128]{4,3,2,1,0:T(8,128)}, f32[2,8,8,16,128]{4,3,2,1,0:T(8,128)S(1)}, u32[]{:S(2)}) copy-start(f32[2,8,8,16,128]{4,3,2,1,0:T(8,128)S(1)} %collective-permute-done.1.refs_7_.refs_17_.refs_8_.refs_18_) | copy-start | bytes 3145732
  90.0 18.4 %collective-permute-start.13 = (f32[4,8,16,128]{3,2,1,0:T(8,128)S(1)}, f32[4,8,16,128]{3,2,1,0:T(8,128)S(1)}, u32[]{:S(2)}, u32[]{:S(2)}) collective-permute-start(f32[4,8,16,128]{3,2,1,0:T(8,128)S(1)} %collective-permute-done.12.refs_11_), channel_id=1, source_target_pairs={{0,16},{16,0},{1,17},{17,1},{2,18},{18,2},{3,19},{19,3},{4,20},{20... | collective-permute-start | bytes 786440 | tf_op jit(solution)/shard_map/ppermute | solution.py:209
  91.5 1.0 copy-start.10
  91.5 22.5 %collective-permute-start.15 = (f32[4,8,16,128]{3,2,1,0:T(8,128)S(1)}, f32[4,8,16,128]{3,2,1,0:T(8,128)S(1)}, u32[]{:S(2)}, u32[]{:S(2)}) collective-permute-start(f32[4,8,16,128]{3,2,1,0:T(8,128)S(1)} %collective-permute-done.14.refs_1_), channel_id=1, source_target_pairs={{0,16},{16,0},{1,17},{17,1},{2,18},{18,2},{3,19},{19,3},{4,20},{20... | collective-permute-start | bytes 786440 | tf_op jit(solution)/shard_map/ppermute | solution.py:209
  92.5 1.0 copy-start.11
  93.5 23.5 %collective-permute-start.17 = (f32[4,8,16,128]{3,2,1,0:T(8,128)S(1)}, f32[4,8,16,128]{3,2,1,0:T(8,128)S(1)}, u32[]{:S(2)}, u32[]{:S(2)}) collective-permute-start(f32[4,8,16,128]{3,2,1,0:T(8,128)S(1)} %collective-permute-done.16.refs_11_), channel_id=1, source_target_pairs={{0,16},{16,0},{1,17},{17,1},{2,18},{18,2},{3,19},{19,3},{4,20},{20... | collective-permute-start | bytes 786440 | tf_op jit(solution)/shard_map/ppermute | solution.py:209
  120.4 1.2 collective-permute-start.18
  121.7 3.7 %collective-permute-start.19 = (f32[32,64]{1,0:T(8,128)S(1)}, f32[32,64]{1,0:T(8,128)S(1)}, u32[]{:S(2)}, u32[]{:S(2)}) collective-permute-start(f32[32,64]{1,0:T(8,128)S(1)} %bitcast_add_fusion), channel_id=1, source_target_pairs={{0,2},{1,3},{2,0},{3,1},{4,6},{5,7},{6,4},{7,5},{8,10},{9,11},{10,... | collective-permute-start | bytes 24584 | tf_op jit(solution)/shard_map/ppermute | solution.py:225
  125.4 3.7 %collective-permute-start.20 = (f32[32,64]{1,0:T(8,128)S(1)}, f32[32,64]{1,0:T(8,128)S(1)}, u32[]{:S(2)}, u32[]{:S(2)}) collective-permute-start(f32[32,64]{1,0:T(8,128)S(1)} %add.30), channel_id=1, source_target_pairs={{0,4},{1,5},{2,6},{3,7},{4,0},{5,1},{6,2},{7,3},{8,12},{9,13},{10,... | collective-permute-start | bytes 24584 | tf_op jit(solution)/shard_map/ppermute | solution.py:225
  129.2 4.6 %collective-permute-start.21 = (f32[32,64]{1,0:T(8,128)S(1)}, f32[32,64]{1,0:T(8,128)S(1)}, u32[]{:S(2)}, u32[]{:S(2)}) collective-permute-start(f32[32,64]{1,0:T(8,128)S(1)} %add.31), channel_id=1, source_target_pairs={{0,8},{1,9},{2,10},{3,11},{4,12},{5,13},{6,14},{7,15},{8,0},{9,1},... | collective-permute-start | bytes 24584 | tf_op jit(solution)/shard_map/ppermute | solution.py:225

commit v2 on v1

v2 whole, which is shorter than its diff:
```python
import functools
import jax
import jax.numpy as jnp
from jax import lax
from jax.experimental import pallas as pl
from jax.experimental.pallas import tpu as pltpu
from jax.sharding import PartitionSpec as P

F32 = jnp.float32
BF16 = jnp.bfloat16
SUB = 8
START = (6, 1, 2, 3, 7, 4, 5)
USE = (1, 6, 2, 3, 7, 4, 5)
BLOCK = 16
NT = (((1,), (1,)), ((), ()))
NN = (((1,), (0,)), ((), ()))


def entry_slot(slots, owner, core, entry):
    probe = slots[2 * owner + core]
    return jnp.where(probe < 0, 1 - entry, entry)


def chip_list(slots, chip, cap):
    found = []
    for core in range(2):
        owner = chip * 2 + core
        found.append([slots[2 * owner + entry_slot(slots, owner, core, e)] for e in range(2)])
    if cap == 4:
        return found[0] + found[1]
    return [found[0][0], jnp.maximum(found[0][1], found[1][0]), found[1][1]]


def split(x):
    high = x.astype(BF16)
    return high, (x - high.astype(F32)).astype(BF16)


def pack_kernel(chips, cap, share, slots, place, query, own, *rest):
    sends, sem = rest[:-1], rest[-1]
    chip, group = place[0], place[2]
    start = pl.multiple_of(group * share, share)
    copies = []
    for d in range(1, chips):
        for k, module in enumerate(chip_list(slots, chip ^ d, cap)):
            source = query.at[jnp.maximum(module, 0), pl.ds(start, share)]
            copies.append(pltpu.make_async_copy(source, sends[d - 1].at[k], sem))
    for k, module in enumerate(chip_list(slots, chip, cap)):
        copies.append(pltpu.make_async_copy(query.at[jnp.maximum(module, 0)], own.at[k], sem))
    for copy in copies:
        copy.start()
    for copy in copies:
        copy.wait()


def pack(chips, cap, share, slots, place, query):
    _, count, rows, width = query.shape
    vmem = pl.BlockSpec(memory_space=pltpu.VMEM)
    return pl.pallas_call(
        functools.partial(pack_kernel, chips, cap, share),
        grid_spec=pltpu.PrefetchScalarGridSpec(
            num_scalar_prefetch=2,
            grid=(),
            in_specs=[pl.BlockSpec(memory_space=pltpu.HBM)],
            out_specs=[vmem] * chips,
            scratch_shapes=[pltpu.SemaphoreType.DMA],
        ),
        out_shape=[jax.ShapeDtypeStruct((cap, count, rows, width), F32)]
        + [jax.ShapeDtypeStruct((cap, share, rows, width), F32)] * (chips - 1),
        compiler_params=pltpu.CompilerParams(vmem_limit_bytes=8 << 20),
        cost_estimate=pl.CostEstimate(flops=0, bytes_accessed=2 * query.size * 4, transcendentals=0),
        name="pack",
    )(slots, place, query)


def fold_kernel(chips, slots, place, ranks, train, out_basis, in_basis, corrections, mine, other,
                w_in, w_out, w_out_t, w_in_t, weight):
    core = place[1]
    owner = place[0] * 2 + core
    entry = pl.program_id(0)
    block, dim = train.shape[1], train.shape[2]
    rows = dim // (2 * chips)

    @pl.when(pl.program_id(1) == 0)
    def _():
        module = slots[2 * owner + entry_slot(slots, owner, core, entry)]
        rank = jnp.where(module >= 0, ranks[jnp.maximum(module, 0)], 0)
        spectrum = corrections[0]
        damping = 0.1 * (jnp.sum(spectrum) / (dim * dim))
        a = lax.broadcasted_iota(jnp.int32, (dim, dim), 0)
        b = lax.broadcasted_iota(jnp.int32, (dim, dim), 1)
        kept = jnp.where((a < rank) & (b < rank), 1.0 / (spectrum + damping), 0.0)
        weight[...] = kept.T
        for ref, value in ((w_in, in_basis[0]), (w_out, out_basis[0]),
                           (w_out_t, out_basis[0].T), (w_in_t, in_basis[0].T)):
            high, low = split(value)
            both = jnp.concatenate([high, low], axis=1)
            ref[...] = jnp.concatenate([both, both], axis=0)

    def times(x, ref):
        flat = x.reshape(SUB * dim, dim)
        high, low = split(flat)
        product = lax.dot_general(jnp.concatenate([high, low], axis=1), ref[...], NN, preferred_element_type=F32)
        return (product[:, :dim] + product[:, dim:]).reshape(SUB, dim, dim)

    def chain(sub):
        x = times(train[0, sub * SUB:(sub + 1) * SUB], w_in)
        x = times(jnp.swapaxes(x, 1, 2), w_out) * weight[...][None]
        x = jnp.swapaxes(times(x, w_out_t), 1, 2)
        x = jnp.swapaxes(times(x, w_in_t), 0, 1).reshape(chips, 2, rows, SUB, dim)
        place_in = slice(sub * SUB, (sub + 1) * SUB)
        first = core == 0
        mine[0, :, :, place_in] = jnp.where(first, x[:, 0], x[:, 1])
        other[0, :, :, place_in] = jnp.where(first, x[:, 1], x[:, 0])

    for sub in range(block // SUB):
        chain(sub)


def fold(chips, part, parts, slots, place, ranks, train, out_basis, in_basis, corrections):
    entries, examples, dim, _ = train.shape
    rows = dim // (2 * chips)
    size = examples // parts
    block = min(size, BLOCK)
    steps = size // block

    def slot_of(entry, slots, place):
        return entry_slot(slots, place[0] * 2 + place[1], place[1], entry)

    square = pl.BlockSpec((1, dim, dim), lambda n, b, s, p, r: (slot_of(n, s, p), 0, 0))
    out = pl.BlockSpec((1, chips, rows, block, dim), lambda n, b, s, p, r: (n, 0, 0, b, 0))
    shape = jax.ShapeDtypeStruct((entries, chips, rows, size, dim), F32)
    double = pltpu.VMEM((2 * dim, 2 * dim), BF16)
    return pl.pallas_call(
        functools.partial(fold_kernel, chips),
        grid_spec=pltpu.PrefetchScalarGridSpec(
            num_scalar_prefetch=3,
            grid=(entries, steps),
            in_specs=[pl.BlockSpec((1, block, dim, dim), lambda n, b, s, p, r: (slot_of(n, s, p), part * steps + b, 0, 0)),
                      square, square, square],
            out_specs=[out, out],
            scratch_shapes=[double] * 4 + [pltpu.VMEM((dim, dim), F32)],
        ),
        out_shape=[shape, shape],
        compiler_params=pltpu.CompilerParams(vmem_limit_bytes=24 << 20),
        cost_estimate=pl.CostEstimate(flops=entries * size * 8 * dim**3 * 4, bytes_accessed=entries * size * dim * dim * 8, transcendentals=0),
        name="fold",
    )(slots, place, ranks, train, out_basis, in_basis, corrections)


def score_kernel(cap, shifts, groups, share, parts, place, *refs):
    chip, core, group = place[0], place[1], place[2]
    refs = list(refs)
    out = refs.pop()
    previous = refs.pop(0)
    folded = [[refs.pop(0) for _ in range(parts)] for _ in range(2)]
    rows = folded[0][0].shape[2]
    total = None
    for d in shifts:
        if d == 0:
            own = refs.pop(0)
            queries = [own.at[:, pl.ds(pl.multiple_of((group ^ t) * share, share), share)] for t in range(groups)]
        else:
            queries = [refs.pop(0) for _ in range(groups)]
        for side in range(2):
            for entry in range(2):
                position = jnp.where(core == side, 0, cap - 2) + entry
                high, low = split(jnp.concatenate(
                    [jnp.concatenate([q[position, :, r, :] for q in queries], axis=0) for r in range(rows)], axis=1))
                left = jnp.concatenate([high, low], axis=0)
                high, low = split(jnp.concatenate(
                    [jnp.concatenate([g[entry, chip ^ d, r] for g in folded[side]], axis=0) for r in range(rows)], axis=1))
                right = jnp.concatenate([high, low], axis=0)
                product = lax.dot_general(left, right, NT, preferred_element_type=F32)
                total = product if total is None else total + product
    half, examples = total.shape[0] // 2, total.shape[1] // 2
    result = (total[:half, :examples] + total[half:, examples:]) + (total[:half, examples:] + total[half:, :examples])
    for t in range(groups):
        place_out = pl.ds(pl.multiple_of((group ^ t) * share, share), share)
        out[place_out, :] = result[t * share:(t + 1) * share] + previous[place_out, :]


def score(cap, shifts, groups, share, place, previous, queries, folded):
    parts = len(folded[0])
    vmem = pl.BlockSpec(memory_space=pltpu.VMEM)
    operands = [previous] + folded[0] + folded[1]
    for query in queries:
        operands += query
    return pl.pallas_call(
        functools.partial(score_kernel, cap, shifts, groups, share, parts),
        grid_spec=pltpu.PrefetchScalarGridSpec(
            num_scalar_prefetch=1, grid=(), in_specs=[vmem] * len(operands), out_specs=vmem),
        out_shape=jax.ShapeDtypeStruct(previous.shape, F32),
        compiler_params=pltpu.CompilerParams(vmem_limit_bytes=40 << 20),
        cost_estimate=pl.CostEstimate(flops=len(shifts) * 4 * 2 * 64 * 128 * 1024, bytes_accessed=len(shifts) * 1536 * 1024, transcendentals=0),
        name="score",
    )(place, *operands)


def order_of(chips):
    if chips == 8:
        return START, USE
    return (tuple(range(1, chips)),) * 2


def body(devices, groups, cap, query_grads, train_grads, out_basis, in_basis, corrections, ranks, slot_modules):
    chips, parts = devices // 2, 4
    count, examples = query_grads.shape[1], train_grads.shape[1]
    share = count // groups
    index, group = lax.axis_index("module"), lax.axis_index("group")
    place = jnp.stack([index // 2, index % 2, group]).astype(jnp.int32)
    own, *sends = pack(chips, cap, share, slot_modules, place, query_grads)
    start, use = order_of(chips)
    arrived = {0: [own]}
    for d in start:
        arrived[d] = [lax.ppermute(sends[d - 1], "module", [(i, i ^ (2 * d)) for i in range(devices)])]
    for d in use:
        for t in range(1, groups):
            arrived[d].append(lax.ppermute(arrived[d][0], "group", [(i, i ^ t) for i in range(groups)]))
    mine, other = [], []
    for part in range(parts):
        here, there = fold(chips, part, parts, slot_modules, place, ranks, train_grads, out_basis, in_basis, corrections)
        mine.append(here)
        other.append(lax.ppermute(there, "module", [(i, i ^ 1) for i in range(devices)]))
    total = jnp.zeros((count, examples), F32)
    everything = (0,) + use
    cuts = [0, *range(len(everything) - 1, 0, -2)[::-1], len(everything)]
    for first, last in zip(cuts, cuts[1:]):
        shifts = everything[first:last]
        total = score(cap, shifts, groups, share, place, total, [arrived[d] for d in shifts], [mine, other])
    stride = 1
    while stride < devices:
        total = total + lax.ppermute(total, "module", [(i, i ^ stride) for i in range(devices)])
        stride *= 2
    return total


def solution(mesh):
    devices, groups = mesh.shape["module"], mesh.shape["group"]

    def branch(cap, *arrays):
        return body(devices, groups, cap, *arrays)

    def whole(*arrays):
        if devices != 16:
            return branch(4, *arrays)
        fullest = jnp.min(arrays[-1].reshape(-1, 4), axis=1)
        return lax.cond(jnp.max(fullest) < 0, functools.partial(branch, 3), functools.partial(branch, 4), *arrays)

    return jax.shard_map(
        whole,
        mesh=mesh,
        in_specs=(
            P(None, None, "module", None),
            P("module", "group", None, None),
            P("module", None, None),
            P("module", None, None),
            P("module", None, None),
            P(),
            P(),
        ),
        out_specs=P(None, "group"),
        check_vma=False,
    )
```

time: 135 us -> 121 us (0.90)
  Pallas kernels: 46 us -> 27.9 us
  waiting for transfers between devices: 59.3 us -> 69.8 us
  local copies, waits for them, and re-layouts: 6.73 us -> 1.37 us
    pallas_call x4, Pallas kernels: 29.5 us -> 17.3 us  [fold(): pl.pallas_call(functools.partial(fold_kernel, chips), grid_spec=pltpu.Pre...]
    ppermute x7, waiting for transfers between devices: 20.8 us -> 28.6 us  [body(): lax.ppermute(sends[d - 1], 'module', [(i, i ^ 2 * d) for i in range(devic...]
    unnamed x28 -> x2, local copies, waits for them, and re-layouts: 6.17 us -> 0.6 us
    pallas_call x4 -> x5, Pallas kernels: 11.6 us -> 7.51 us  [score(): pl.pallas_call(functools.partial(score_kernel, cap, shifts, groups, share...]
    pallas_call x1, Pallas kernels: 4.95 us -> 3.14 us  [pack(): pl.pallas_call(functools.partial(pack_kernel, chips, cap, share), grid_sp...]
    ppermute x7, waiting for transfers between devices: 26.3 us -> 28 us  [body(): lax.ppermute(arrived[d][0], 'group', [(i, i ^ t) for i in range(groups)])]
  transfers between devices with their start and end apart: 22 -> 22, of which waited for: 12 -> 14; matrix products, arithmetic and copies ran while one was open for 0% -> 0% of each run, Pallas kernels for 28% -> 20%
where the time goes in v2:
time: 121 us
  waiting for transfers between devices  69.8 us (58%)
  Pallas kernels  27.9 us (23%)
  starting transfers between devices  19.7 us (16%)
  local copies, waits for them, and re-layouts  1.37 us (1%)
    ppermute x7, waiting for transfers between devices, body(): lax.ppermute(sends[d - 1], 'module', [(i, i ^ 2 * d) for i in range(devic...  28.6 us
    ppermute x7, waiting for transfers between devices, body(): lax.ppermute(arrived[d][0], 'group', [(i, i ^ t) for i in range(groups)])  28 us
    pallas_call x4, Pallas kernels, fold(): pl.pallas_call(functools.partial(fold_kernel, chips), grid_spec=pltpu.Pre...  17.3 us
    ppermute x4, waiting for transfers between devices, body(): lax.ppermute(total, 'module', [(i, i ^ stride) for i in range(devices)])  13.2 us
    ppermute x7, starting transfers between devices, body(): lax.ppermute(sends[d - 1], 'module', [(i, i ^ 2 * d) for i in range(devic...  9.73 us
    ppermute x7, starting transfers between devices, body(): lax.ppermute(arrived[d][0], 'group', [(i, i ^ t) for i in range(groups)])  9.16 us
    pallas_call x5, Pallas kernels, score(): pl.pallas_call(functools.partial(score_kernel, cap, shifts, groups, share...  7.51 us
    pallas_call x1, Pallas kernels, pack(): pl.pallas_call(functools.partial(pack_kernel, chips, cap, share), grid_sp...  3.14 us
  transfers between devices with their start and end apart: 22, of which 14 were waited for; matrix products, arithmetic and copies ran while one was open for 0% of the time, Pallas kernels for 20%

profile of v2, /device:TPU:0, one launch (start us, length us, event | category | flops | bytes accessed | tf_op | source)
XLA Modules:
  0.0 120.6 jit_solution(2792608016122776271)
XLA Ops:
  0.0 0.7 reshape.3
  0.7 0.1 reduce_min.9
  0.9 0.6 reduce_max.9
  2.1 117.9 %conditional.1 = (f32[32,64]{1,0:T(8,128)S(1)}) conditional(s32[]{:T(128)} %convert_element_type.3, (s32[32]{0:T(128)}, s32[16]{0:T(128)}, f32[2,64,128,128]{3,2,1,0:T(8,128)}, f32[2,128,128]{2,1,0:T(8,128)}, f32[2,128,128]{2,1,0:T(8,128)}, /*index=5*/f32[2,128,128]{2,1,0:T(8,128)}, f32[16,32,8,128]{3,2,1,0:T(8,128)}) %tuple.11, (s32[32]{0:T(128)}, ...), branch_computations={%region_2.3_spmd, %region_3.4_spmd} | conditional | flops 9126813696 | bytes 105097280 | solution.py:248
  2.2 0.0 copy-start.6
  2.2 0.1 pad_add_fusion.place
  2.3 3.1 %pack.2 = (f32[4,32,8,128]{3,2,1,0:T(8,128)S(1)}, f32[4,16,8,128]{3,2,1,0:T(8,128)S(1)}, f32[4,16,8,128]{3,2,1,0:T(8,128)S(1)}, f32[4,16,8,128]{3,2,1,0:T(8,128)...) custom-call(s32[32]{0:T(128)} %get-tuple-element.36.slots, ...), custom_call_target="tpu_custom_call" | custom-call | bytes 4194304 | tf_op jit(solution)/shard_map/cond/branch_0_fun/pack/pallas_call | solution.py:59
  5.5 3.0 %collective-permute-start.4 = (f32[4,16,8,128]{3,2,1,0:T(8,128)S(1)}, f32[4,16,8,128]{3,2,1,0:T(8,128)S(1)}, u32[]{:S(2)}, u32[]{:S(2)}) collective-permute-start(f32[4,16,8,128]{3,2,1,0:T(8,128)S(1)} %get-tuple-element.52), channel_id=1, source_target_pairs={{0,2},{1,3},{2,0},{3,1},{4,6},{5,7},{6,4},{7,5},{8,10},{9,11},{10,... | collective-permute-start | bytes 786440 | tf_op jit(solution)/shard_map/cond/branch_0_fun/ppermute | solution.py:216
  8.4 3.6 %collective-permute-start.6 = (f32[4,16,8,128]{3,2,1,0:T(8,128)S(1)}, f32[4,16,8,128]{3,2,1,0:T(8,128)S(1)}, u32[]{:S(2)}, u32[]{:S(2)}) collective-permute-start(f32[4,16,8,128]{3,2,1,0:T(8,128)S(1)} %get-tuple-element.53), channel_id=1, source_target_pairs={{0,12},{1,13},{2,14},{3,15},{4,8},{5,9},{6,10},{7,11},{8,4},{9,5},... | collective-permute-start | bytes 786440 | tf_op jit(solution)/shard_map/cond/branch_0_fun/ppermute | solution.py:216
  12.0 2.1 %collective-permute-start.8 = (f32[4,16,8,128]{3,2,1,0:T(8,128)S(1)}, f32[4,16,8,128]{3,2,1,0:T(8,128)S(1)}, u32[]{:S(2)}, u32[]{:S(2)}) collective-permute-start(f32[4,16,8,128]{3,2,1,0:T(8,128)S(1)} %get-tuple-element.54), channel_id=1, source_target_pairs={{0,4},{1,5},{2,6},{3,7},{4,0},{5,1},{6,2},{7,3},{8,12},{9,13},{10,... | collective-permute-start | bytes 786440 | tf_op jit(solution)/shard_map/cond/branch_0_fun/ppermute | solution.py:216
  14.1 1.1 collective-permute-start.12
  15.2 5.4 %fold.8 = (f32[2,8,8,16,128]{4,3,2,1,0:T(8,128)S(1)}, f32[2,8,8,16,128]{4,3,2,1,0:T(8,128)S(1)}) custom-call(s32[32]{0:T(128)} %get-tuple-element.36.slots, s32[3]{0:T(128)S(1)} %pad_add_fusion.place, s32[16]{0:T(128)} %get-tuple-element.37.ranks, f32[2,64,128,128]{3,2,1,0:T(8,128)} %get-tuple-element.38.train, f32[2,128,128]{2,1,0:T(8,128)} %get-tuple-element.39.out_basis, ...), custom_call_target="tpu_custom_call" | custom-call | flops 2147483648 | bytes 4194304 | tf_op jit(solution)/shard_map/cond/branch_0_fun/fold/pallas_call | solution.py:134
  20.7 4.0 %fold.9 = (f32[2,8,8,16,128]{4,3,2,1,0:T(8,128)S(1)}, f32[2,8,8,16,128]{4,3,2,1,0:T(8,128)S(1)}) custom-call(s32[32]{0:T(128)S(1)} %copy-done.9, s32[3]{0:T(128)S(1)} %pad_add_fusion.place, s32[16]{0:T(128)S(1)} %copy-done.11, f32[2,64,128,128]{3,2,1,0:T(8,128)S(1)} %copy-done, f32[2,128,128]{2,1,0:T(8,128)S(1)} %copy-done.2, f32[2,128,128]{2,1,0:T(8,128)S(1)} %copy-done.4, ...), custom_call_target="tpu_custom_call" | custom-call | flops 2147483648 | bytes 4194304 | tf_op jit(solution)/shard_map/cond/branch_0_fun/fold/pallas_call | solution.py:134
  24.7 4.0 %fold.10 = (f32[2,8,8,16,128]{4,3,2,1,0:T(8,128)S(1)}, f32[2,8,8,16,128]{4,3,2,1,0:T(8,128)S(1)}) custom-call(s32[32]{0:T(128)S(1)} %copy-done.9, s32[3]{0:T(128)S(1)} %pad_add_fusion.place, s32[16]{0:T(128)S(1)} %copy-done.11, f32[2,64,128,128]{3,2,1,0:T(8,128)S(1)} %copy-done, f32[2,128,128]{2,1,0:T(8,128)S(1)} %copy-done.2, f32[2,128,128]{2,1,0:T(8,128)S(1)} %copy-done.4, ...), custom_call_target="tpu_custom_call" | custom-call | flops 2147483648 | bytes 4194304 | tf_op jit(solution)/shard_map/cond/branch_0_fun/fold/pallas_call | solution.py:134
  28.6 0.1 collective-permute-start
  28.7 0.5 collective-permute-start.1
  29.2 0.1 collective-permute-start.2
  29.3 4.9 %collective-permute-done.8.refs_9_ = f32[4,16,8,128]{3,2,1,0:T(8,128)S(1)} collective-permute-done((f32[4,16,8,128]{3,2,1,0:T(8,128)S(1)}, f32[4,16,8,128]{3,2,1,0:T(8,128)S(1)}, u32[]{:S(2)}, u32[]{:S(2)}) %collective-permute-start.8) | collective-permute-done | bytes 262176 | tf_op jit(solution)/shard_map/cond/branch_0_fun/ppermute | solution.py:216
  34.2 4.0 %fold.11 = (f32[2,8,8,16,128]{4,3,2,1,0:T(8,128)S(1)}, f32[2,8,8,16,128]{4,3,2,1,0:T(8,128)S(1)}) custom-call(s32[32]{0:T(128)S(1)} %copy-done.9, s32[3]{0:T(128)S(1)} %pad_add_fusion.place, s32[16]{0:T(128)S(1)} %copy-done.11, f32[2,64,128,128]{3,2,1,0:T(8,128)S(1)} %copy-done, f32[2,128,128]{2,1,0:T(8,128)S(1)} %copy-done.2, f32[2,128,128]{2,1,0:T(8,128)S(1)} %copy-done.4, ...), custom_call_target="tpu_custom_call" | custom-call | flops 2147483648 | bytes 4194304 | tf_op jit(solution)/shard_map/cond/branch_0_fun/fold/pallas_call | solution.py:134
  38.2 0.1 collective-permute-start.3
  38.2 8.9 %collective-permute-done.14.refs_11_ = f32[4,16,8,128]{3,2,1,0:T(8,128)S(1)} collective-permute-done((f32[4,16,8,128]{3,2,1,0:T(8,128)S(1)}, f32[4,16,8,128]{3,2,1,0:T(8,128)S(1)}, u32[]{:S(2)}, u32[]{:S(2)}) %collective-permute-start.14) | collective-permute-done | bytes 262176 | tf_op jit(solution)/shard_map/cond/branch_0_fun/ppermute | solution.py:216
  47.1 14.8 %collective-permute-done.16.refs_9_ = f32[4,16,8,128]{3,2,1,0:T(8,128)S(1)} collective-permute-done((f32[4,16,8,128]{3,2,1,0:T(8,128)S(1)}, f32[4,16,8,128]{3,2,1,0:T(8,128)S(1)}, u32[]{:S(2)}, u32[]{:S(2)}) %collective-permute-start.16) | collective-permute-done | bytes 262176 | tf_op jit(solution)/shard_map/cond/branch_0_fun/ppermute | solution.py:216
  62.0 1.7 %collective-permute-start.5 = (f32[4,16,8,128]{3,2,1,0:T(8,128)S(1)}, f32[4,16,8,128]{3,2,1,0:T(8,128)S(1)}, u32[]{:S(2)}, u32[]{:S(2)}) collective-permute-start(f32[4,16,8,128]{3,2,1,0:T(8,128)S(1)} %collective-permute-done.4.refs_9_), channel_id=1, source_target_pairs={{0,16},{16,0},{1,17},{17,1},{2,18},{18,2},{3,19},{19,3},{4,20},{20... | collective-permute-start | bytes 786440 | tf_op jit(solution)/shard_map/cond/branch_0_fun/ppermute | solution.py:219
  63.6 6.2 %collective-permute-done.5.refs_10_ = f32[4,16,8,128]{3,2,1,0:T(8,128)S(1)} collective-permute-done((f32[4,16,8,128]{3,2,1,0:T(8,128)S(1)}, f32[4,16,8,128]{3,2,1,0:T(8,128)S(1)}, u32[]{:S(2)}, u32[]{:S(2)}) %collective-permute-start.5) | collective-permute-done | bytes 262176 | tf_op jit(solution)/shard_map/cond/branch_0_fun/ppermute | solution.py:219
  69.8 1.7 %collective-permute-start.7 = (f32[4,16,8,128]{3,2,1,0:T(8,128)S(1)}, f32[4,16,8,128]{3,2,1,0:T(8,128)S(1)}, u32[]{:S(2)}, u32[]{:S(2)}) collective-permute-start(f32[4,16,8,128]{3,2,1,0:T(8,128)S(1)} %collective-permute-done.6.refs_11_), channel_id=1, source_target_pairs={{0,16},{16,0},{1,17},{17,1},{2,18},{18,2},{3,19},{19,3},{4,20},{20... | collective-permute-start | bytes 786440 | tf_op jit(solution)/shard_map/cond/branch_0_fun/ppermute | solution.py:219
  71.5 5.3 %collective-permute-done.7.refs_12_ = f32[4,16,8,128]{3,2,1,0:T(8,128)S(1)} collective-permute-done((f32[4,16,8,128]{3,2,1,0:T(8,128)S(1)}, f32[4,16,8,128]{3,2,1,0:T(8,128)S(1)}, u32[]{:S(2)}, u32[]{:S(2)}) %collective-permute-start.7) | collective-permute-done | bytes 262176 | tf_op jit(solution)/shard_map/cond/branch_0_fun/ppermute | solution.py:219
  76.8 1.7 %collective-permute-start.11 = (f32[4,16,8,128]{3,2,1,0:T(8,128)S(1)}, f32[4,16,8,128]{3,2,1,0:T(8,128)S(1)}, u32[]{:S(2)}, u32[]{:S(2)}) collective-permute-start(f32[4,16,8,128]{3,2,1,0:T(8,128)S(1)} %collective-permute-done.10.refs_11_), channel_id=1, source_target_pairs={{0,16},{16,0},{1,17},{17,1},{2,18},{18,2},{3,19},{19,3},{4,20},{20... | collective-permute-start | bytes 786440 | tf_op jit(solution)/shard_map/cond/branch_0_fun/ppermute | solution.py:219
  78.5 0.3 collective-permute-start.9
  78.8 1.7 %collective-permute-start.13 = (f32[4,16,8,128]{3,2,1,0:T(8,128)S(1)}, f32[4,16,8,128]{3,2,1,0:T(8,128)S(1)}, u32[]{:S(2)}, u32[]{:S(2)}) collective-permute-start(f32[4,16,8,128]{3,2,1,0:T(8,128)S(1)} %collective-permute-done.12.refs_9_), channel_id=1, source_target_pairs={{0,16},{16,0},{1,17},{17,1},{2,18},{18,2},{3,19},{19,3},{4,20},{20... | collective-permute-start | bytes 786440 | tf_op jit(solution)/shard_map/cond/branch_0_fun/ppermute | solution.py:219
  80.6 0.3 collective-permute-start.15
  80.9 1.7 %collective-permute-start.17 = (f32[4,16,8,128]{3,2,1,0:T(8,128)S(1)}, f32[4,16,8,128]{3,2,1,0:T(8,128)S(1)}, u32[]{:S(2)}, u32[]{:S(2)}) collective-permute-start(f32[4,16,8,128]{3,2,1,0:T(8,128)S(1)} %collective-permute-done.16.refs_9_), channel_id=1, source_target_pairs={{0,16},{16,0},{1,17},{17,1},{2,18},{18,2},{3,19},{19,3},{4,20},{20... | collective-permute-start | bytes 786440 | tf_op jit(solution)/shard_map/cond/branch_0_fun/ppermute | solution.py:219
  82.6 1.2 %score.10.refs_0_ = f32[32,64]{1,0:T(8,128)S(1)} custom-call(s32[3]{0:T(128)S(1)} %pad_add_fusion.place, f32[32,64]{1,0:T(8,128)S(1)} %broadcast_1_refs_0_.0.refs_0_, f32[2,8,8,16,128]{4,3,2,1,0:T(8,128)S(1)} %get-tuple-element.42.refs_1_, f32[2,8,8,16,128]{4,3,2,1,0:T(8,128)S(1)} %get-tuple-element.43.refs_2_, ...), custom_call_target="tpu_custom_call" | custom-call | flops 67108864 | bytes 1572864 | tf_op jit(solution)/shard_map/cond/branch_0_fun/score/pallas_call | solution.py:189
  83.8 1.7 %score.11.refs_0_ = f32[32,64]{1,0:T(8,128)S(1)} custom-call(s32[3]{0:T(128)S(1)} %pad_add_fusion.place, f32[32,64]{1,0:T(8,128)S(1)} %score.10.refs_0_, f32[2,8,8,16,128]{4,3,2,1,0:T(8,128)S(1)} %get-tuple-element.42.refs_1_, f32[2,8,8,16,128]{4,3,2,1,0:T(8,128)S(1)} %get-tuple-element.43.refs_2_, f32[2,8,8,16,128]{4,3,2,1,0:T(8,128)S(1)} %get-tuple-element.44.refs_3_, ...), custom_call_target="tpu_custom_call" | custom-call | flops 134217728 | bytes 3145728 | tf_op jit(solution)/shard_map/cond/branch_0_fun/score/pallas_call | solution.py:189
  85.5 0.5 collective-permute-done.11.refs_12_
  86.0 5.6 %collective-permute-done.9.refs_10_ = f32[4,16,8,128]{3,2,1,0:T(8,128)S(1)} collective-permute-done((f32[4,16,8,128]{3,2,1,0:T(8,128)S(1)}, f32[4,16,8,128]{3,2,1,0:T(8,128)S(1)}, u32[]{:S(2)}, u32[]{:S(2)}) %collective-permute-start.9) | collective-permute-done | bytes 262176 | tf_op jit(solution)/shard_map/cond/branch_0_fun/ppermute | solution.py:219
  91.6 1.7 %score.12.refs_0_ = f32[32,64]{1,0:T(8,128)S(1)} custom-call(s32[3]{0:T(128)S(1)} %pad_add_fusion.place, f32[32,64]{1,0:T(8,128)S(1)} %score.11.refs_0_, f32[2,8,8,16,128]{4,3,2,1,0:T(8,128)S(1)} %get-tuple-element.42.refs_1_, f32[2,8,8,16,128]{4,3,2,1,0:T(8,128)S(1)} %get-tuple-element.43.refs_2_, f32[2,8,8,16,128]{4,3,2,1,0:T(8,128)S(1)} %get-tuple-element.44.refs_3_, ...), custom_call_target="tpu_custom_call" | custom-call | flops 134217728 | bytes 3145728 | tf_op jit(solution)/shard_map/cond/branch_0_fun/score/pallas_call | solution.py:189
  93.3 3.9 %collective-permute-done.13.refs_10_ = f32[4,16,8,128]{3,2,1,0:T(8,128)S(1)} collective-permute-done((f32[4,16,8,128]{3,2,1,0:T(8,128)S(1)}, f32[4,16,8,128]{3,2,1,0:T(8,128)S(1)}, u32[]{:S(2)}, u32[]{:S(2)}) %collective-permute-start.13) | collective-permute-done | bytes 262176 | tf_op jit(solution)/shard_map/cond/branch_0_fun/ppermute | solution.py:219
  97.2 5.4 %collective-permute-done.15.refs_12_ = f32[4,16,8,128]{3,2,1,0:T(8,128)S(1)} collective-permute-done((f32[4,16,8,128]{3,2,1,0:T(8,128)S(1)}, f32[4,16,8,128]{3,2,1,0:T(8,128)S(1)}, u32[]{:S(2)}, u32[]{:S(2)}) %collective-permute-start.15) | collective-permute-done | bytes 262176 | tf_op jit(solution)/shard_map/cond/branch_0_fun/ppermute | solution.py:219
  102.6 1.7 %score.13.refs_0_ = f32[32,64]{1,0:T(8,128)S(1)} custom-call(s32[3]{0:T(128)S(1)} %pad_add_fusion.place, f32[32,64]{1,0:T(8,128)S(1)} %score.12.refs_0_, f32[2,8,8,16,128]{4,3,2,1,0:T(8,128)S(1)} %get-tuple-element.42.refs_1_, f32[2,8,8,16,128]{4,3,2,1,0:T(8,128)S(1)} %get-tuple-element.43.refs_2_, f32[2,8,8,16,128]{4,3,2,1,0:T(8,128)S(1)} %get-tuple-element.44.refs_3_, ...), custom_call_target="tpu_custom_call" | custom-call | flops 134217728 | bytes 3145728 | tf_op jit(solution)/shard_map/cond/branch_0_fun/score/pallas_call | solution.py:189
  104.3 1.1 collective-permute-done.17.refs_10_
  105.4 1.2 %score.14 = f32[32,64]{1,0:T(8,128)S(1)} custom-call(s32[3]{0:T(128)S(1)} %pad_add_fusion.place, f32[32,64]{1,0:T(8,128)S(1)} %score.13.refs_0_, f32[2,8,8,16,128]{4,3,2,1,0:T(8,128)S(1)} %get-tuple-element.42.refs_1_, f32[2,8,8,16,128]{4,3,2,1,0:T(8,128)S(1)} %get-tuple-element.43.refs_2_, f32[2,8,8,16,128]{4,3,2,1,0:T(8,128)S(1)} %get-tuple-element.44.refs_3_, ...), custom_call_target="tpu_custom_call" | custom-call | flops 67108864 | bytes 1572864 | tf_op jit(solution)/shard_map/cond/branch_0_fun/score/pallas_call | solution.py:189
  106.7 0.0 collective-permute-start.18
  106.7 1.2 collective-permute-done.18
  107.9 3.7 %collective-permute-done.19 = f32[32,64]{1,0:T(8,128)S(1)} collective-permute-done((f32[32,64]{1,0:T(8,128)S(1)}, f32[32,64]{1,0:T(8,128)S(1)}, u32[]{:S(2)}, u32[]{:S(2)}) %collective-permute-start.19) | collective-permute-done | bytes 8224 | tf_op jit(solution)/shard_map/cond/branch_0_fun/ppermute | solution.py:233
  111.6 3.7 %collective-permute-done.20 = f32[32,64]{1,0:T(8,128)S(1)} collective-permute-done((f32[32,64]{1,0:T(8,128)S(1)}, f32[32,64]{1,0:T(8,128)S(1)}, u32[]{:S(2)}, u32[]{:S(2)}) %collective-permute-start.20) | collective-permute-done | bytes 8224 | tf_op jit(solution)/shard_map/cond/branch_0_fun/ppermute | solution.py:233
  115.4 0.1 collective-permute-start.21
  115.5 4.5 %collective-permute-done.21 = f32[32,64]{1,0:T(8,128)S(1)} collective-permute-done((f32[32,64]{1,0:T(8,128)S(1)}, f32[32,64]{1,0:T(8,128)S(1)}, u32[]{:S(2)}, u32[]{:S(2)}) %collective-permute-start.21) | collective-permute-done | bytes 8224 | tf_op jit(solution)/shard_map/cond/branch_0_fun/ppermute | solution.py:233
  120.0 0.6 copy-done.13
  (30 shorter events, 0.1 us)
Async XLA Ops:
  2.2 18.5 %copy-start.2 = (f32[2,128,128]{2,1,0:T(8,128)S(1)}, f32[2,128,128]{2,1,0:T(8,128)}, u32[]{:S(2)}) copy-start(f32[2,128,128]{2,1,0:T(8,128)} %get-tuple-element.39.out_basis) | copy-start | bytes 393220 | tf_op jit(solution)/shard_map/cond
  2.2 18.5 %copy-start.4 = (f32[2,128,128]{2,1,0:T(8,128)S(1)}, f32[2,128,128]{2,1,0:T(8,128)}, u32[]{:S(2)}) copy-start(f32[2,128,128]{2,1,0:T(8,128)} %get-tuple-element.40.in_basis) | copy-start | bytes 393220 | tf_op jit(solution)/shard_map/cond
  2.2 18.5 %copy-start.6 = (f32[2,128,128]{2,1,0:T(8,128)S(1)}, f32[2,128,128]{2,1,0:T(8,128)}, u32[]{:S(2)}) copy-start(f32[2,128,128]{2,1,0:T(8,128)} %get-tuple-element.41.corrections) | copy-start | bytes 393220 | tf_op jit(solution)/shard_map/cond
  2.2 18.5 %copy-start.9 = (s32[32]{0:T(128)S(1)}, s32[32]{0:T(128)}, u32[]{:S(2)}) copy-start(s32[32]{0:T(128)} %get-tuple-element.36.slots) | copy-start | bytes 388 | tf_op jit(solution)/shard_map/cond
  2.2 18.5 %copy-start.11 = (s32[16]{0:T(128)S(1)}, s32[16]{0:T(128)}, u32[]{:S(2)}) copy-start(s32[16]{0:T(128)} %get-tuple-element.37.ranks) | copy-start | bytes 196 | tf_op jit(solution)/shard_map/cond
  2.2 18.5 %copy-start = (f32[2,64,128,128]{3,2,1,0:T(8,128)S(1)}, f32[2,64,128,128]{3,2,1,0:T(8,128)}, u32[]{:S(2)}) copy-start(f32[2,64,128,128]{3,2,1,0:T(8,128)} %get-tuple-element.38.train) | copy-start | bytes 25165828 | tf_op jit(solution)/shard_map/cond
  5.5 23.2 %collective-permute-start.4 = (f32[4,16,8,128]{3,2,1,0:T(8,128)S(1)}, f32[4,16,8,128]{3,2,1,0:T(8,128)S(1)}, u32[]{:S(2)}, u32[]{:S(2)}) collective-permute-start(f32[4,16,8,128]{3,2,1,0:T(8,128)S(1)} %get-tuple-element.52), channel_id=1, source_target_pairs={{0,2},{1,3},{2,0},{3,1},{4,6},{5,7},{6,4},{7,5},{8,10},{9,11},{10,... | collective-permute-start | bytes 786440 | tf_op jit(solution)/shard_map/cond/branch_0_fun/ppermute | solution.py:216
  8.4 20.3 %collective-permute-start.6 = (f32[4,16,8,128]{3,2,1,0:T(8,128)S(1)}, f32[4,16,8,128]{3,2,1,0:T(8,128)S(1)}, u32[]{:S(2)}, u32[]{:S(2)}) collective-permute-start(f32[4,16,8,128]{3,2,1,0:T(8,128)S(1)} %get-tuple-element.53), channel_id=1, source_target_pairs={{0,12},{1,13},{2,14},{3,15},{4,8},{5,9},{6,10},{7,11},{8,4},{9,5},... | collective-permute-start | bytes 786440 | tf_op jit(solution)/shard_map/cond/branch_0_fun/ppermute | solution.py:216
  12.0 17.2 %collective-permute-start.10 = (f32[4,16,8,128]{3,2,1,0:T(8,128)S(1)}, f32[4,16,8,128]{3,2,1,0:T(8,128)S(1)}, u32[]{:S(2)}, u32[]{:S(2)}) collective-permute-start(f32[4,16,8,128]{3,2,1,0:T(8,128)S(1)} %get-tuple-element.55), channel_id=1, source_target_pairs={{0,6},{1,7},{2,4},{3,5},{4,2},{5,3},{6,0},{7,1},{8,14},{9,15},{10,... | collective-permute-start | bytes 786440 | tf_op jit(solution)/shard_map/cond/branch_0_fun/ppermute | solution.py:216
  12.0 22.2 %collective-permute-start.8 = (f32[4,16,8,128]{3,2,1,0:T(8,128)S(1)}, f32[4,16,8,128]{3,2,1,0:T(8,128)S(1)}, u32[]{:S(2)}, u32[]{:S(2)}) collective-permute-start(f32[4,16,8,128]{3,2,1,0:T(8,128)S(1)} %get-tuple-element.54), channel_id=1, source_target_pairs={{0,4},{1,5},{2,6},{3,7},{4,0},{5,1},{6,2},{7,3},{8,12},{9,13},{10,... | collective-permute-start | bytes 786440 | tf_op jit(solution)/shard_map/cond/branch_0_fun/ppermute | solution.py:216
  14.1 24.1 %collective-permute-start.12 = (f32[4,16,8,128]{3,2,1,0:T(8,128)S(1)}, f32[4,16,8,128]{3,2,1,0:T(8,128)S(1)}, u32[]{:S(2)}, u32[]{:S(2)}) collective-permute-start(f32[4,16,8,128]{3,2,1,0:T(8,128)S(1)} %get-tuple-element.56), channel_id=1, source_target_pairs={{0,14},{1,15},{2,12},{3,13},{4,10},{5,11},{6,8},{7,9},{8,6},{9,7},... | collective-permute-start | bytes 786440 | tf_op jit(solution)/shard_map/cond/branch_0_fun/ppermute | solution.py:216
  28.6 49.9 %collective-permute-start = (f32[2,8,8,16,128]{4,3,2,1,0:T(8,128)S(1)}, f32[2,8,8,16,128]{4,3,2,1,0:T(8,128)S(1)}, u32[]{:S(2)}, u32[]{:S(2)}) collective-permute-start(f32[2,8,8,16,128]{4,3,2,1,0:T(8,128)S(1)} %get-tuple-element.46), channel_id=1, source_target_pairs={{0,1},{1,0},{2,3},{3,2},{4,5},{5,4},{6,7},{7,6},{8,9},{9,8},{10,11... | collective-permute-start | bytes 3145736 | tf_op jit(solution)/shard_map/cond/branch_0_fun/ppermute | solution.py:224
  28.7 50.1 %collective-permute-start.1 = (f32[2,8,8,16,128]{4,3,2,1,0:T(8,128)S(1)}, f32[2,8,8,16,128]{4,3,2,1,0:T(8,128)S(1)}, u32[]{:S(2)}, u32[]{:S(2)}) collective-permute-start(f32[2,8,8,16,128]{4,3,2,1,0:T(8,128)S(1)} %get-tuple-element.47), channel_id=1, source_target_pairs={{0,1},{1,0},{2,3},{3,2},{4,5},{5,4},{6,7},{7,6},{8,9},{9,8},{10,11... | collective-permute-start | bytes 3145736 | tf_op jit(solution)/shard_map/cond/branch_0_fun/ppermute | solution.py:224
  29.2 51.4 %collective-permute-start.2 = (f32[2,8,8,16,128]{4,3,2,1,0:T(8,128)S(1)}, f32[2,8,8,16,128]{4,3,2,1,0:T(8,128)S(1)}, u32[]{:S(2)}, u32[]{:S(2)}) collective-permute-start(f32[2,8,8,16,128]{4,3,2,1,0:T(8,128)S(1)} %get-tuple-element.48), channel_id=1, source_target_pairs={{0,1},{1,0},{2,3},{3,2},{4,5},{5,4},{6,7},{7,6},{8,9},{9,8},{10,11... | collective-permute-start | bytes 3145736 | tf_op jit(solution)/shard_map/cond/branch_0_fun/ppermute | solution.py:224
  34.2 12.9 %collective-permute-start.14 = (f32[4,16,8,128]{3,2,1,0:T(8,128)S(1)}, f32[4,16,8,128]{3,2,1,0:T(8,128)S(1)}, u32[]{:S(2)}, u32[]{:S(2)}) collective-permute-start(f32[4,16,8,128]{3,2,1,0:T(8,128)S(1)} %get-tuple-element.57), channel_id=1, source_target_pairs={{0,8},{1,9},{2,10},{3,11},{4,12},{5,13},{6,14},{7,15},{8,0},{9,1},... | collective-permute-start | bytes 786440 | tf_op jit(solution)/shard_map/cond/branch_0_fun/ppermute | solution.py:216
  38.2 42.7 %collective-permute-start.3 = (f32[2,8,8,16,128]{4,3,2,1,0:T(8,128)S(1)}, f32[2,8,8,16,128]{4,3,2,1,0:T(8,128)S(1)}, u32[]{:S(2)}, u32[]{:S(2)}) collective-permute-start(f32[2,8,8,16,128]{4,3,2,1,0:T(8,128)S(1)} %get-tuple-element.49), channel_id=1, source_target_pairs={{0,1},{1,0},{2,3},{3,2},{4,5},{5,4},{6,7},{7,6},{8,9},{9,8},{10,11... | collective-permute-start | bytes 3145736 | tf_op jit(solution)/shard_map/cond/branch_0_fun/ppermute | solution.py:224
  47.1 14.8 %collective-permute-start.16 = (f32[4,16,8,128]{3,2,1,0:T(8,128)S(1)}, f32[4,16,8,128]{3,2,1,0:T(8,128)S(1)}, u32[]{:S(2)}, u32[]{:S(2)}) collective-permute-start(f32[4,16,8,128]{3,2,1,0:T(8,128)S(1)} %get-tuple-element.58), channel_id=1, source_target_pairs={{0,10},{1,11},{2,8},{3,9},{4,14},{5,15},{6,12},{7,13},{8,2},{9,3},... | collective-permute-start | bytes 786440 | tf_op jit(solution)/shard_map/cond/branch_0_fun/ppermute | solution.py:216
  62.0 7.9 %collective-permute-start.5 = (f32[4,16,8,128]{3,2,1,0:T(8,128)S(1)}, f32[4,16,8,128]{3,2,1,0:T(8,128)S(1)}, u32[]{:S(2)}, u32[]{:S(2)}) collective-permute-start(f32[4,16,8,128]{3,2,1,0:T(8,128)S(1)} %collective-permute-done.4.refs_9_), channel_id=1, source_target_pairs={{0,16},{16,0},{1,17},{17,1},{2,18},{18,2},{3,19},{19,3},{4,20},{20... | collective-permute-start | bytes 786440 | tf_op jit(solution)/shard_map/cond/branch_0_fun/ppermute | solution.py:219
  69.8 7.0 %collective-permute-start.7 = (f32[4,16,8,128]{3,2,1,0:T(8,128)S(1)}, f32[4,16,8,128]{3,2,1,0:T(8,128)S(1)}, u32[]{:S(2)}, u32[]{:S(2)}) collective-permute-start(f32[4,16,8,128]{3,2,1,0:T(8,128)S(1)} %collective-permute-done.6.refs_11_), channel_id=1, source_target_pairs={{0,16},{16,0},{1,17},{17,1},{2,18},{18,2},{3,19},{19,3},{4,20},{20... | collective-permute-start | bytes 786440 | tf_op jit(solution)/shard_map/cond/branch_0_fun/ppermute | solution.py:219
  76.8 9.2 %collective-permute-start.11 = (f32[4,16,8,128]{3,2,1,0:T(8,128)S(1)}, f32[4,16,8,128]{3,2,1,0:T(8,128)S(1)}, u32[]{:S(2)}, u32[]{:S(2)}) collective-permute-start(f32[4,16,8,128]{3,2,1,0:T(8,128)S(1)} %collective-permute-done.10.refs_11_), channel_id=1, source_target_pairs={{0,16},{16,0},{1,17},{17,1},{2,18},{18,2},{3,19},{19,3},{4,20},{20... | collective-permute-start | bytes 786440 | tf_op jit(solution)/shard_map/cond/branch_0_fun/ppermute | solution.py:219
  78.5 13.1 %collective-permute-start.9 = (f32[4,16,8,128]{3,2,1,0:T(8,128)S(1)}, f32[4,16,8,128]{3,2,1,0:T(8,128)S(1)}, u32[]{:S(2)}, u32[]{:S(2)}) collective-permute-start(f32[4,16,8,128]{3,2,1,0:T(8,128)S(1)} %collective-permute-done.8.refs_9_), channel_id=1, source_target_pairs={{0,16},{16,0},{1,17},{17,1},{2,18},{18,2},{3,19},{19,3},{4,20},{20... | collective-permute-start | bytes 786440 | tf_op jit(solution)/shard_map/cond/branch_0_fun/ppermute | solution.py:219
  78.8 18.4 %collective-permute-start.13 = (f32[4,16,8,128]{3,2,1,0:T(8,128)S(1)}, f32[4,16,8,128]{3,2,1,0:T(8,128)S(1)}, u32[]{:S(2)}, u32[]{:S(2)}) collective-permute-start(f32[4,16,8,128]{3,2,1,0:T(8,128)S(1)} %collective-permute-done.12.refs_9_), channel_id=1, source_target_pairs={{0,16},{16,0},{1,17},{17,1},{2,18},{18,2},{3,19},{19,3},{4,20},{20... | collective-permute-start | bytes 786440 | tf_op jit(solution)/shard_map/cond/branch_0_fun/ppermute | solution.py:219
  80.6 22.1 %collective-permute-start.15 = (f32[4,16,8,128]{3,2,1,0:T(8,128)S(1)}, f32[4,16,8,128]{3,2,1,0:T(8,128)S(1)}, u32[]{:S(2)}, u32[]{:S(2)}) collective-permute-start(f32[4,16,8,128]{3,2,1,0:T(8,128)S(1)} %collective-permute-done.14.refs_11_), channel_id=1, source_target_pairs={{0,16},{16,0},{1,17},{17,1},{2,18},{18,2},{3,19},{19,3},{4,20},{20... | collective-permute-start | bytes 786440 | tf_op jit(solution)/shard_map/cond/branch_0_fun/ppermute | solution.py:219
  80.9 24.6 %collective-permute-start.17 = (f32[4,16,8,128]{3,2,1,0:T(8,128)S(1)}, f32[4,16,8,128]{3,2,1,0:T(8,128)S(1)}, u32[]{:S(2)}, u32[]{:S(2)}) collective-permute-start(f32[4,16,8,128]{3,2,1,0:T(8,128)S(1)} %collective-permute-done.16.refs_9_), channel_id=1, source_target_pairs={{0,16},{16,0},{1,17},{17,1},{2,18},{18,2},{3,19},{19,3},{4,20},{20... | collective-permute-start | bytes 786440 | tf_op jit(solution)/shard_map/cond/branch_0_fun/ppermute | solution.py:219
  106.7 1.2 collective-permute-start.18
  107.9 3.7 %collective-permute-start.19 = (f32[32,64]{1,0:T(8,128)S(1)}, f32[32,64]{1,0:T(8,128)S(1)}, u32[]{:S(2)}, u32[]{:S(2)}) collective-permute-start(f32[32,64]{1,0:T(8,128)S(1)} %add.24), channel_id=1, source_target_pairs={{0,2},{1,3},{2,0},{3,1},{4,6},{5,7},{6,4},{7,5},{8,10},{9,11},{10,... | collective-permute-start | bytes 24584 | tf_op jit(solution)/shard_map/cond/branch_0_fun/ppermute | solution.py:233
  111.6 3.7 %collective-permute-start.20 = (f32[32,64]{1,0:T(8,128)S(1)}, f32[32,64]{1,0:T(8,128)S(1)}, u32[]{:S(2)}, u32[]{:S(2)}) collective-permute-start(f32[32,64]{1,0:T(8,128)S(1)} %add.25), channel_id=1, source_target_pairs={{0,4},{1,5},{2,6},{3,7},{4,0},{5,1},{6,2},{7,3},{8,12},{9,13},{10,... | collective-permute-start | bytes 24584 | tf_op jit(solution)/shard_map/cond/branch_0_fun/ppermute | solution.py:233
  115.4 4.6 %collective-permute-start.21 = (f32[32,64]{1,0:T(8,128)S(1)}, f32[32,64]{1,0:T(8,128)S(1)}, u32[]{:S(2)}, u32[]{:S(2)}) collective-permute-start(f32[32,64]{1,0:T(8,128)S(1)} %add.26), channel_id=1, source_target_pairs={{0,8},{1,9},{2,10},{3,11},{4,12},{5,13},{6,14},{7,15},{8,0},{9,1},... | collective-permute-start | bytes 24584 | tf_op jit(solution)/shard_map/cond/branch_0_fun/ppermute | solution.py:233
  120.0 0.6 copy-start.13

commit v3 on v2

--- a/solution.py
+++ b/solution.py
@@ -31,6 +31,10 @@
     return [found[0][0], jnp.maximum(found[0][1], found[1][0]), found[1][1]]
 
 
+def tail_of():
+    return 0
+
+
 def split(x):
     high = x.astype(BF16)
     return high, (x - high.astype(F32)).astype(BF16)
@@ -40,11 +44,20 @@
     sends, sem = rest[:-1], rest[-1]
     chip, group = place[0], place[2]
     start = pl.multiple_of(group * share, share)
+    tail = tail_of()
+    half = share // 2
     copies = []
     for d in range(1, chips):
         for k, module in enumerate(chip_list(slots, chip ^ d, cap)):
-            source = query.at[jnp.maximum(module, 0), pl.ds(start, share)]
-            copies.append(pltpu.make_async_copy(source, sends[d - 1].at[k], sem))
+            source = query.at[jnp.maximum(module, 0)]
+            if d != tail:
+                copies.append(pltpu.make_async_copy(source.at[pl.ds(start, share)], sends[d - 1].at[k], sem))
+                continue
+            copies.append(pltpu.make_async_copy(source.at[pl.ds(start, half)], sends[d - 1].at[k], sem))
+            for t in range(2):
+                late = pl.multiple_of((group ^ t) * share + half, half)
+                copies.append(pltpu.make_async_copy(
+                    source.at[pl.ds(late, half)], sends[chips - 1].at[k, pl.ds(t * half, half)], sem))
     for k, module in enumerate(chip_list(slots, chip, cap)):
         copies.append(pltpu.make_async_copy(query.at[jnp.maximum(module, 0)], own.at[k], sem))
     for copy in copies:
@@ -56,17 +69,18 @@
 def pack(chips, cap, share, slots, place, query):
     _, count, rows, width = query.shape
     vmem = pl.BlockSpec(memory_space=pltpu.VMEM)
+    tail = tail_of()
+    sizes = [count] + [share // 2 if d == tail else share for d in range(1, chips)] + [share] * (tail > 0)
     return pl.pallas_call(
         functools.partial(pack_kernel, chips, cap, share),
         grid_spec=pltpu.PrefetchScalarGridSpec(
             num_scalar_prefetch=2,
             grid=(),
             in_specs=[pl.BlockSpec(memory_space=pltpu.HBM)],
-            out_specs=[vmem] * chips,
+            out_specs=[vmem] * len(sizes),
             scratch_shapes=[pltpu.SemaphoreType.DMA],
         ),
-        out_shape=[jax.ShapeDtypeStruct((cap, count, rows, width), F32)]
-        + [jax.ShapeDtypeStruct((cap, share, rows, width), F32)] * (chips - 1),
+        out_shape=[jax.ShapeDtypeStruct((cap, size, rows, width), F32) for size in sizes],
         compiler_params=pltpu.CompilerParams(vmem_limit_bytes=8 << 20),
         cost_estimate=pl.CostEstimate(flops=0, bytes_accessed=2 * query.size * 4, transcendentals=0),
         name="pack",
@@ -162,17 +176,32 @@
             queries = [own.at[:, pl.ds(pl.multiple_of((group ^ t) * share, share), share)] for t in range(groups)]
         else:
             queries = [refs.pop(0) for _ in range(groups)]
-        for side in range(2):
-            for entry in range(2):
-                position = jnp.where(core == side, 0, cap - 2) + entry
-                high, low = split(jnp.concatenate(
-                    [jnp.concatenate([q[position, :, r, :] for q in queries], axis=0) for r in range(rows)], axis=1))
-                left = jnp.concatenate([high, low], axis=0)
-                high, low = split(jnp.concatenate(
-                    [jnp.concatenate([g[entry, chip ^ d, r] for g in folded[side]], axis=0) for r in range(rows)], axis=1))
-                right = jnp.concatenate([high, low], axis=0)
-                product = lax.dot_general(left, right, NT, preferred_element_type=F32)
-                total = product if total is None else total + product
+        late = refs.pop(0) if d and d == tail_of() else None
+
+        def query_rows(position, r):
+            found = []
+            for t, q in enumerate(queries):
+                found.append(q[position, :, r, :])
+                if late is not None:
+                    found.append(late[position, t * (share // 2):(t + 1) * (share // 2), r, :])
+            return jnp.concatenate(found, axis=0)
+
+        def grads(side, entry):
+            return jnp.concatenate(
+                [jnp.concatenate([g[entry, chip ^ d, r] for g in folded[side]], axis=0) for r in range(rows)], axis=1)
+
+        if cap == 4:
+            work = [(core * 2, grads(0, 0)), (core * 2 + 1, grads(0, 1)),
+                    (2 - core * 2, grads(1, 0)), (3 - core * 2, grads(1, 1))]
+        else:
+            work = [(core * 2, grads(0, core)), (1, grads(0, 1 - core) + grads(1, core)), (2 - core * 2, grads(1, 1 - core))]
+        for position, block in work:
+            high, low = split(jnp.concatenate([query_rows(position, r) for r in range(rows)], axis=1))
+            left = jnp.concatenate([high, low], axis=0)
+            high, low = split(block)
+            right = jnp.concatenate([high, low], axis=0)
+            product = lax.dot_general(left, right, NT, preferred_element_type=F32)
+            total = product if total is None else total + product
     half, examples = total.shape[0] // 2, total.shape[1] // 2
     result = (total[:half, :examples] + total[half:, examples:]) + (total[:half, examples:] + total[half:, :examples])
     for t in range(groups):
@@ -214,9 +243,14 @@
     arrived = {0: [own]}
     for d in start:
         arrived[d] = [lax.ppermute(sends[d - 1], "module", [(i, i ^ (2 * d)) for i in range(devices)])]
+    tail = tail_of()
+    if tail:
+        late = lax.ppermute(sends[-1], "module", [(i, i ^ (2 * tail)) for i in range(devices)])
     for d in use:
         for t in range(1, groups):
             arrived[d].append(lax.ppermute(arrived[d][0], "group", [(i, i ^ t) for i in range(groups)]))
+    if tail:
+        arrived[tail].append(late)
     mine, other = [], []
     for part in range(parts):
         here, there = fold(chips, part, parts, slot_modules, place, ranks, train_grads, out_basis, in_basis, corrections)
@@ -230,8 +264,9 @@
         total = score(cap, shifts, groups, share, place, total, [arrived[d] for d in shifts], [mine, other])
     stride = 1
     while stride < devices:
-        total = total + lax.ppermute(total, "module", [(i, i ^ stride) for i in range(devices)])
-        stride *= 2
+        radix = 4 if 1 < stride and stride * 2 < devices else 2
+        total += sum(lax.ppermute(total, "module", [(i, i ^ (stride * t)) for i in range(devices)]) for t in range(1, radix))
+        stride *= radix
     return total
 
 
@@ -244,8 +279,9 @@
     def whole(*arrays):
         if devices != 16:
             return branch(4, *arrays)
-        fullest = jnp.min(arrays[-1].reshape(-1, 4), axis=1)
-        return lax.cond(jnp.max(fullest) < 0, functools.partial(branch, 3), functools.partial(branch, 4), *arrays)
+        slots = arrays[-1]
+        counts = jnp.sum(jnp.where(slots >= 0, 1 << (3 * (lax.iota(jnp.int32, slots.shape[0]) // 4)), 0))
+        return lax.cond((counts & 0o44444444) == 0, functools.partial(branch, 3), functools.partial(branch, 4), *arrays)
 
     return jax.shard_map(
         whole,

time: 121 us -> 118 us (0.975)
  waiting for transfers between devices: 69.8 us -> 61.6 us
  starting transfers between devices: 19.7 us -> 25.8 us
    ppermute x4 -> x5, waiting for transfers between devices: 13.2 us -> 5 us  [body(): lax.ppermute(total, 'module', [(i, i ^ stride * t) for i in range(devices)])]
    ppermute x4 -> x5, starting transfers between devices: 0.14 us -> 6.2 us  [body(): lax.ppermute(total, 'module', [(i, i ^ stride * t) for i in range(devices)])]
    reduce_sum x0 -> x1, other arithmetic: none -> 1.29 us  [whole(): jnp.sum(jnp.where(slots >= 0, 1 << 3 * (lax.iota(jnp.int32, slots.shape[0...]
  transfers between devices with their start and end apart: 22 -> 23, of which waited for: 14 -> 15; matrix products, arithmetic and copies ran while one was open for 0% -> 0% of each run, Pallas kernels for 20% -> 20%
where the time goes in v3:
time: 118 us
  waiting for transfers between devices  61.6 us (52%)
  Pallas kernels  28 us (24%)
  starting transfers between devices  25.8 us (22%)
  other arithmetic  1.39 us (1%)
    ppermute x7, waiting for transfers between devices, body(): lax.ppermute(sends[d - 1], 'module', [(i, i ^ 2 * d) for i in range(devic...  28.6 us
    ppermute x7, waiting for transfers between devices, body(): lax.ppermute(arrived[d][0], 'group', [(i, i ^ t) for i in range(groups)])  28 us
    pallas_call x4, Pallas kernels, fold(): pl.pallas_call(functools.partial(fold_kernel, chips), grid_spec=pltpu.Pre...  17.3 us
    ppermute x7, starting transfers between devices, body(): lax.ppermute(sends[d - 1], 'module', [(i, i ^ 2 * d) for i in range(devic...  9.73 us
    ppermute x7, starting transfers between devices, body(): lax.ppermute(arrived[d][0], 'group', [(i, i ^ t) for i in range(groups)])  9.16 us
    pallas_call x5, Pallas kernels, score(): pl.pallas_call(functools.partial(score_kernel, cap, shifts, groups, share...  7.51 us
    ppermute x5, starting transfers between devices, body(): lax.ppermute(total, 'module', [(i, i ^ stride * t) for i in range(devices)])  6.2 us
    ppermute x5, waiting for transfers between devices, body(): lax.ppermute(total, 'module', [(i, i ^ stride * t) for i in range(devices)])  5 us
  transfers between devices with their start and end apart: 23, of which 15 were waited for; matrix products, arithmetic and copies ran while one was open for 0% of the time, Pallas kernels for 20%

profile of v3, /device:TPU:0, one launch (start us, length us, event | category | flops | bytes accessed | tf_op | source)
XLA Modules:
  0.0 118.3 jit_solution(2596923087874599557)
XLA Ops:
  0.0 1.3 %fusion.2 = s32[]{:T(128)} fusion(s32[32]{0:T(128)} %param.15), kind=kLoop, calls=%fused_computation.11 | loop fusion | flops 415 | bytes 132 | tf_op jit(solution)/shard_map/reduce_sum | solution.py:283
  1.9 115.8 %conditional.1 = (f32[32,64]{1,0:T(8,128)S(1)}) conditional(s32[]{:T(128)} %convert_element_type.3, (s32[32]{0:T(128)}, s32[16]{0:T(128)}, f32[2,64,128,128]{3,2,1,0:T(8,128)}, f32[2,128,128]{2,1,0:T(8,128)}, f32[2,128,128]{2,1,0:T(8,128)}, /*index=5*/f32[2,128,128]{2,1,0:T(8,128)}, f32[16,32,8,128]{3,2,1,0:T(8,128)}) %tuple.11, (s32[32]{0:T(128)}, ...), branch_computations={%region_1.2_spmd, %region_2.3_spmd} | conditional | flops 9126815744 | bytes 105121896 | solution.py:284
  2.1 0.1 pad_add_fusion.place
  2.1 3.1 %pack.2 = (f32[4,32,8,128]{3,2,1,0:T(8,128)S(1)}, f32[4,16,8,128]{3,2,1,0:T(8,128)S(1)}, f32[4,16,8,128]{3,2,1,0:T(8,128)S(1)}, f32[4,16,8,128]{3,2,1,0:T(8,128)...) custom-call(s32[32]{0:T(128)} %get-tuple-element.36.slots, ...), custom_call_target="tpu_custom_call" | custom-call | bytes 4194304 | tf_op jit(solution)/shard_map/cond/branch_0_fun/pack/pallas_call | solution.py:74
  5.3 3.0 %collective-permute-start.4 = (f32[4,16,8,128]{3,2,1,0:T(8,128)S(1)}, f32[4,16,8,128]{3,2,1,0:T(8,128)S(1)}, u32[]{:S(2)}, u32[]{:S(2)}) collective-permute-start(f32[4,16,8,128]{3,2,1,0:T(8,128)S(1)} %get-tuple-element.52), channel_id=1, source_target_pairs={{0,2},{1,3},{2,0},{3,1},{4,6},{5,7},{6,4},{7,5},{8,10},{9,11},{10,... | collective-permute-start | bytes 786440 | tf_op jit(solution)/shard_map/cond/branch_0_fun/ppermute | solution.py:245
  8.3 3.6 %collective-permute-start.6 = (f32[4,16,8,128]{3,2,1,0:T(8,128)S(1)}, f32[4,16,8,128]{3,2,1,0:T(8,128)S(1)}, u32[]{:S(2)}, u32[]{:S(2)}) collective-permute-start(f32[4,16,8,128]{3,2,1,0:T(8,128)S(1)} %get-tuple-element.53), channel_id=1, source_target_pairs={{0,12},{1,13},{2,14},{3,15},{4,8},{5,9},{6,10},{7,11},{8,4},{9,5},... | collective-permute-start | bytes 786440 | tf_op jit(solution)/shard_map/cond/branch_0_fun/ppermute | solution.py:245
  11.8 2.1 %collective-permute-start.8 = (f32[4,16,8,128]{3,2,1,0:T(8,128)S(1)}, f32[4,16,8,128]{3,2,1,0:T(8,128)S(1)}, u32[]{:S(2)}, u32[]{:S(2)}) collective-permute-start(f32[4,16,8,128]{3,2,1,0:T(8,128)S(1)} %get-tuple-element.54), channel_id=1, source_target_pairs={{0,4},{1,5},{2,6},{3,7},{4,0},{5,1},{6,2},{7,3},{8,12},{9,13},{10,... | collective-permute-start | bytes 786440 | tf_op jit(solution)/shard_map/cond/branch_0_fun/ppermute | solution.py:245
  13.9 1.1 collective-permute-start.12
  15.0 5.4 %fold.8 = (f32[2,8,8,16,128]{4,3,2,1,0:T(8,128)S(1)}, f32[2,8,8,16,128]{4,3,2,1,0:T(8,128)S(1)}) custom-call(s32[32]{0:T(128)} %get-tuple-element.36.slots, s32[3]{0:T(128)S(1)} %pad_add_fusion.place, s32[16]{0:T(128)} %get-tuple-element.37.ranks, f32[2,64,128,128]{3,2,1,0:T(8,128)} %get-tuple-element.38.train, f32[2,128,128]{2,1,0:T(8,128)} %get-tuple-element.39.out_basis, ...), custom_call_target="tpu_custom_call" | custom-call | flops 2147483648 | bytes 4194304 | tf_op jit(solution)/shard_map/cond/branch_0_fun/fold/pallas_call | solution.py:148
  20.5 4.0 %fold.9 = (f32[2,8,8,16,128]{4,3,2,1,0:T(8,128)S(1)}, f32[2,8,8,16,128]{4,3,2,1,0:T(8,128)S(1)}) custom-call(s32[32]{0:T(128)S(1)} %copy-done.9, s32[3]{0:T(128)S(1)} %pad_add_fusion.place, s32[16]{0:T(128)S(1)} %copy-done.11, f32[2,64,128,128]{3,2,1,0:T(8,128)S(1)} %copy-done, f32[2,128,128]{2,1,0:T(8,128)S(1)} %copy-done.2, f32[2,128,128]{2,1,0:T(8,128)S(1)} %copy-done.4, ...), custom_call_target="tpu_custom_call" | custom-call | flops 2147483648 | bytes 4194304 | tf_op jit(solution)/shard_map/cond/branch_0_fun/fold/pallas_call | solution.py:148
  24.5 4.0 %fold.10 = (f32[2,8,8,16,128]{4,3,2,1,0:T(8,128)S(1)}, f32[2,8,8,16,128]{4,3,2,1,0:T(8,128)S(1)}) custom-call(s32[32]{0:T(128)S(1)} %copy-done.9, s32[3]{0:T(128)S(1)} %pad_add_fusion.place, s32[16]{0:T(128)S(1)} %copy-done.11, f32[2,64,128,128]{3,2,1,0:T(8,128)S(1)} %copy-done, f32[2,128,128]{2,1,0:T(8,128)S(1)} %copy-done.2, f32[2,128,128]{2,1,0:T(8,128)S(1)} %copy-done.4, ...), custom_call_target="tpu_custom_call" | custom-call | flops 2147483648 | bytes 4194304 | tf_op jit(solution)/shard_map/cond/branch_0_fun/fold/pallas_call | solution.py:148
  28.4 0.1 collective-permute-start
  28.5 0.5 collective-permute-start.1
  29.0 0.1 collective-permute-start.2
  29.1 4.9 %collective-permute-done.8.refs_9_ = f32[4,16,8,128]{3,2,1,0:T(8,128)S(1)} collective-permute-done((f32[4,16,8,128]{3,2,1,0:T(8,128)S(1)}, f32[4,16,8,128]{3,2,1,0:T(8,128)S(1)}, u32[]{:S(2)}, u32[]{:S(2)}) %collective-permute-start.8) | collective-permute-done | bytes 262176 | tf_op jit(solution)/shard_map/cond/branch_0_fun/ppermute | solution.py:245
  34.0 4.0 %fold.11 = (f32[2,8,8,16,128]{4,3,2,1,0:T(8,128)S(1)}, f32[2,8,8,16,128]{4,3,2,1,0:T(8,128)S(1)}) custom-call(s32[32]{0:T(128)S(1)} %copy-done.9, s32[3]{0:T(128)S(1)} %pad_add_fusion.place, s32[16]{0:T(128)S(1)} %copy-done.11, f32[2,64,128,128]{3,2,1,0:T(8,128)S(1)} %copy-done, f32[2,128,128]{2,1,0:T(8,128)S(1)} %copy-done.2, f32[2,128,128]{2,1,0:T(8,128)S(1)} %copy-done.4, ...), custom_call_target="tpu_custom_call" | custom-call | flops 2147483648 | bytes 4194304 | tf_op jit(solution)/shard_map/cond/branch_0_fun/fold/pallas_call | solution.py:148
  38.0 0.1 collective-permute-start.3
  38.0 8.9 %collective-permute-done.14.refs_11_ = f32[4,16,8,128]{3,2,1,0:T(8,128)S(1)} collective-permute-done((f32[4,16,8,128]{3,2,1,0:T(8,128)S(1)}, f32[4,16,8,128]{3,2,1,0:T(8,128)S(1)}, u32[]{:S(2)}, u32[]{:S(2)}) %collective-permute-start.14) | collective-permute-done | bytes 262176 | tf_op jit(solution)/shard_map/cond/branch_0_fun/ppermute | solution.py:245
  46.9 14.8 %collective-permute-done.16.refs_9_ = f32[4,16,8,128]{3,2,1,0:T(8,128)S(1)} collective-permute-done((f32[4,16,8,128]{3,2,1,0:T(8,128)S(1)}, f32[4,16,8,128]{3,2,1,0:T(8,128)S(1)}, u32[]{:S(2)}, u32[]{:S(2)}) %collective-permute-start.16) | collective-permute-done | bytes 262176 | tf_op jit(solution)/shard_map/cond/branch_0_fun/ppermute | solution.py:245
  61.8 1.7 %collective-permute-start.5 = (f32[4,16,8,128]{3,2,1,0:T(8,128)S(1)}, f32[4,16,8,128]{3,2,1,0:T(8,128)S(1)}, u32[]{:S(2)}, u32[]{:S(2)}) collective-permute-start(f32[4,16,8,128]{3,2,1,0:T(8,128)S(1)} %collective-permute-done.4.refs_9_), channel_id=1, source_target_pairs={{0,16},{16,0},{1,17},{17,1},{2,18},{18,2},{3,19},{19,3},{4,20},{20... | collective-permute-start | bytes 786440 | tf_op jit(solution)/shard_map/cond/branch_0_fun/ppermute | solution.py:251
  63.4 6.2 %collective-permute-done.5.refs_10_ = f32[4,16,8,128]{3,2,1,0:T(8,128)S(1)} collective-permute-done((f32[4,16,8,128]{3,2,1,0:T(8,128)S(1)}, f32[4,16,8,128]{3,2,1,0:T(8,128)S(1)}, u32[]{:S(2)}, u32[]{:S(2)}) %collective-permute-start.5) | collective-permute-done | bytes 262176 | tf_op jit(solution)/shard_map/cond/branch_0_fun/ppermute | solution.py:251
  69.6 1.7 %collective-permute-start.7 = (f32[4,16,8,128]{3,2,1,0:T(8,128)S(1)}, f32[4,16,8,128]{3,2,1,0:T(8,128)S(1)}, u32[]{:S(2)}, u32[]{:S(2)}) collective-permute-start(f32[4,16,8,128]{3,2,1,0:T(8,128)S(1)} %collective-permute-done.6.refs_11_), channel_id=1, source_target_pairs={{0,16},{16,0},{1,17},{17,1},{2,18},{18,2},{3,19},{19,3},{4,20},{20... | collective-permute-start | bytes 786440 | tf_op jit(solution)/shard_map/cond/branch_0_fun/ppermute | solution.py:251
  71.3 5.3 %collective-permute-done.7.refs_12_ = f32[4,16,8,128]{3,2,1,0:T(8,128)S(1)} collective-permute-done((f32[4,16,8,128]{3,2,1,0:T(8,128)S(1)}, f32[4,16,8,128]{3,2,1,0:T(8,128)S(1)}, u32[]{:S(2)}, u32[]{:S(2)}) %collective-permute-start.7) | collective-permute-done | bytes 262176 | tf_op jit(solution)/shard_map/cond/branch_0_fun/ppermute | solution.py:251
  76.6 1.7 %collective-permute-start.11 = (f32[4,16,8,128]{3,2,1,0:T(8,128)S(1)}, f32[4,16,8,128]{3,2,1,0:T(8,128)S(1)}, u32[]{:S(2)}, u32[]{:S(2)}) collective-permute-start(f32[4,16,8,128]{3,2,1,0:T(8,128)S(1)} %collective-permute-done.10.refs_11_), channel_id=1, source_target_pairs={{0,16},{16,0},{1,17},{17,1},{2,18},{18,2},{3,19},{19,3},{4,20},{20... | collective-permute-start | bytes 786440 | tf_op jit(solution)/shard_map/cond/branch_0_fun/ppermute | solution.py:251
  78.3 0.3 collective-permute-start.9
  78.6 1.7 %collective-permute-start.13 = (f32[4,16,8,128]{3,2,1,0:T(8,128)S(1)}, f32[4,16,8,128]{3,2,1,0:T(8,128)S(1)}, u32[]{:S(2)}, u32[]{:S(2)}) collective-permute-start(f32[4,16,8,128]{3,2,1,0:T(8,128)S(1)} %collective-permute-done.12.refs_9_), channel_id=1, source_target_pairs={{0,16},{16,0},{1,17},{17,1},{2,18},{18,2},{3,19},{19,3},{4,20},{20... | collective-permute-start | bytes 786440 | tf_op jit(solution)/shard_map/cond/branch_0_fun/ppermute | solution.py:251
  80.4 0.3 collective-permute-start.15
  80.7 1.7 %collective-permute-start.17 = (f32[4,16,8,128]{3,2,1,0:T(8,128)S(1)}, f32[4,16,8,128]{3,2,1,0:T(8,128)S(1)}, u32[]{:S(2)}, u32[]{:S(2)}) collective-permute-start(f32[4,16,8,128]{3,2,1,0:T(8,128)S(1)} %collective-permute-done.16.refs_9_), channel_id=1, source_target_pairs={{0,16},{16,0},{1,17},{17,1},{2,18},{18,2},{3,19},{19,3},{4,20},{20... | collective-permute-start | bytes 786440 | tf_op jit(solution)/shard_map/cond/branch_0_fun/ppermute | solution.py:251
  82.4 1.2 %score.10.refs_0_ = f32[32,64]{1,0:T(8,128)S(1)} custom-call(s32[3]{0:T(128)S(1)} %pad_add_fusion.place, f32[32,64]{1,0:T(8,128)S(1)} %broadcast_1_refs_0_.0.refs_0_, f32[2,8,8,16,128]{4,3,2,1,0:T(8,128)S(1)} %get-tuple-element.42.refs_1_, f32[2,8,8,16,128]{4,3,2,1,0:T(8,128)S(1)} %get-tuple-element.43.refs_2_, ...), custom_call_target="tpu_custom_call" | custom-call | flops 67108864 | bytes 1572864 | tf_op jit(solution)/shard_map/cond/branch_0_fun/score/pallas_call | solution.py:218
  83.6 1.7 %score.11.refs_0_ = f32[32,64]{1,0:T(8,128)S(1)} custom-call(s32[3]{0:T(128)S(1)} %pad_add_fusion.place, f32[32,64]{1,0:T(8,128)S(1)} %score.10.refs_0_, f32[2,8,8,16,128]{4,3,2,1,0:T(8,128)S(1)} %get-tuple-element.42.refs_1_, f32[2,8,8,16,128]{4,3,2,1,0:T(8,128)S(1)} %get-tuple-element.43.refs_2_, f32[2,8,8,16,128]{4,3,2,1,0:T(8,128)S(1)} %get-tuple-element.44.refs_3_, ...), custom_call_target="tpu_custom_call" | custom-call | flops 134217728 | bytes 3145728 | tf_op jit(solution)/shard_map/cond/branch_0_fun/score/pallas_call | solution.py:218
  85.3 0.5 collective-permute-done.11.refs_12_
  85.8 5.6 %collective-permute-done.9.refs_10_ = f32[4,16,8,128]{3,2,1,0:T(8,128)S(1)} collective-permute-done((f32[4,16,8,128]{3,2,1,0:T(8,128)S(1)}, f32[4,16,8,128]{3,2,1,0:T(8,128)S(1)}, u32[]{:S(2)}, u32[]{:S(2)}) %collective-permute-start.9) | collective-permute-done | bytes 262176 | tf_op jit(solution)/shard_map/cond/branch_0_fun/ppermute | solution.py:251
  91.4 1.7 %score.12.refs_0_ = f32[32,64]{1,0:T(8,128)S(1)} custom-call(s32[3]{0:T(128)S(1)} %pad_add_fusion.place, f32[32,64]{1,0:T(8,128)S(1)} %score.11.refs_0_, f32[2,8,8,16,128]{4,3,2,1,0:T(8,128)S(1)} %get-tuple-element.42.refs_1_, f32[2,8,8,16,128]{4,3,2,1,0:T(8,128)S(1)} %get-tuple-element.43.refs_2_, f32[2,8,8,16,128]{4,3,2,1,0:T(8,128)S(1)} %get-tuple-element.44.refs_3_, ...), custom_call_target="tpu_custom_call" | custom-call | flops 134217728 | bytes 3145728 | tf_op jit(solution)/shard_map/cond/branch_0_fun/score/pallas_call | solution.py:218
  93.1 3.9 %collective-permute-done.13.refs_10_ = f32[4,16,8,128]{3,2,1,0:T(8,128)S(1)} collective-permute-done((f32[4,16,8,128]{3,2,1,0:T(8,128)S(1)}, f32[4,16,8,128]{3,2,1,0:T(8,128)S(1)}, u32[]{:S(2)}, u32[]{:S(2)}) %collective-permute-start.13) | collective-permute-done | bytes 262176 | tf_op jit(solution)/shard_map/cond/branch_0_fun/ppermute | solution.py:251
  97.0 5.4 %collective-permute-done.15.refs_12_ = f32[4,16,8,128]{3,2,1,0:T(8,128)S(1)} collective-permute-done((f32[4,16,8,128]{3,2,1,0:T(8,128)S(1)}, f32[4,16,8,128]{3,2,1,0:T(8,128)S(1)}, u32[]{:S(2)}, u32[]{:S(2)}) %collective-permute-start.15) | collective-permute-done | bytes 262176 | tf_op jit(solution)/shard_map/cond/branch_0_fun/ppermute | solution.py:251
  102.4 1.7 %score.13.refs_0_ = f32[32,64]{1,0:T(8,128)S(1)} custom-call(s32[3]{0:T(128)S(1)} %pad_add_fusion.place, f32[32,64]{1,0:T(8,128)S(1)} %score.12.refs_0_, f32[2,8,8,16,128]{4,3,2,1,0:T(8,128)S(1)} %get-tuple-element.42.refs_1_, f32[2,8,8,16,128]{4,3,2,1,0:T(8,128)S(1)} %get-tuple-element.43.refs_2_, f32[2,8,8,16,128]{4,3,2,1,0:T(8,128)S(1)} %get-tuple-element.44.refs_3_, ...), custom_call_target="tpu_custom_call" | custom-call | flops 134217728 | bytes 3145728 | tf_op jit(solution)/shard_map/cond/branch_0_fun/score/pallas_call | solution.py:218
  104.1 1.1 collective-permute-done.17.refs_10_
  105.2 1.2 %score.14 = f32[32,64]{1,0:T(8,128)S(1)} custom-call(s32[3]{0:T(128)S(1)} %pad_add_fusion.place, f32[32,64]{1,0:T(8,128)S(1)} %score.13.refs_0_, f32[2,8,8,16,128]{4,3,2,1,0:T(8,128)S(1)} %get-tuple-element.42.refs_1_, f32[2,8,8,16,128]{4,3,2,1,0:T(8,128)S(1)} %get-tuple-element.43.refs_2_, f32[2,8,8,16,128]{4,3,2,1,0:T(8,128)S(1)} %get-tuple-element.44.refs_3_, ...), custom_call_target="tpu_custom_call" | custom-call | flops 67108864 | bytes 1572864 | tf_op jit(solution)/shard_map/cond/branch_0_fun/score/pallas_call | solution.py:218
  106.5 0.0 collective-permute-start.18
  106.5 1.2 collective-permute-done.18
  107.7 0.1 collective-permute-start.20
  107.8 3.4 %collective-permute-start.21 = (f32[32,64]{1,0:T(8,128)S(1)}, f32[32,64]{1,0:T(8,128)S(1)}, u32[]{:S(2)}, u32[]{:S(2)}) collective-permute-start(f32[32,64]{1,0:T(8,128)S(1)} %add.29), channel_id=1, source_target_pairs={{0,6},{1,7},{2,4},{3,5},{4,2},{5,3},{6,0},{7,1},{8,14},{9,15},{10,... | collective-permute-start | bytes 24584 | tf_op jit(solution)/shard_map/cond/branch_0_fun/ppermute | solution.py:268
  111.2 0.2 collective-permute-done.19
  111.4 0.1 collective-permute-done.20
  111.5 1.6 %collective-permute-done.21 = f32[32,64]{1,0:T(8,128)S(1)} collective-permute-done((f32[32,64]{1,0:T(8,128)S(1)}, f32[32,64]{1,0:T(8,128)S(1)}, u32[]{:S(2)}, u32[]{:S(2)}) %collective-permute-start.21) | collective-permute-done | bytes 8224 | tf_op jit(solution)/shard_map/cond/branch_0_fun/ppermute | solution.py:268
  113.1 2.7 %collective-permute-start.22 = (f32[32,64]{1,0:T(8,128)S(1)}, f32[32,64]{1,0:T(8,128)S(1)}, u32[]{:S(2)}, u32[]{:S(2)}) collective-permute-start(f32[32,64]{1,0:T(8,128)S(1)} %add_add_fusion), channel_id=1, source_target_pairs={{0,8},{1,9},{2,10},{3,11},{4,12},{5,13},{6,14},{7,15},{8,0},{9,1},... | collective-permute-start | bytes 24584 | tf_op jit(solution)/shard_map/cond/branch_0_fun/ppermute | solution.py:268
  115.8 1.9 %collective-permute-done.22 = f32[32,64]{1,0:T(8,128)S(1)} collective-permute-done((f32[32,64]{1,0:T(8,128)S(1)}, f32[32,64]{1,0:T(8,128)S(1)}, u32[]{:S(2)}, u32[]{:S(2)}) %collective-permute-start.22) | collective-permute-done | bytes 8224 | tf_op jit(solution)/shard_map/cond/branch_0_fun/ppermute | solution.py:268
  117.7 0.6 copy-done.13
  (29 shorter events, 0.1 us)
Async XLA Ops:
  2.0 18.5 %copy-start.2 = (f32[2,128,128]{2,1,0:T(8,128)S(1)}, f32[2,128,128]{2,1,0:T(8,128)}, u32[]{:S(2)}) copy-start(f32[2,128,128]{2,1,0:T(8,128)} %get-tuple-element.39.out_basis) | copy-start | bytes 393220 | tf_op jit(solution)/shard_map/cond
  2.0 18.5 %copy-start.4 = (f32[2,128,128]{2,1,0:T(8,128)S(1)}, f32[2,128,128]{2,1,0:T(8,128)}, u32[]{:S(2)}) copy-start(f32[2,128,128]{2,1,0:T(8,128)} %get-tuple-element.40.in_basis) | copy-start | bytes 393220 | tf_op jit(solution)/shard_map/cond
  2.0 18.5 %copy-start.6 = (f32[2,128,128]{2,1,0:T(8,128)S(1)}, f32[2,128,128]{2,1,0:T(8,128)}, u32[]{:S(2)}) copy-start(f32[2,128,128]{2,1,0:T(8,128)} %get-tuple-element.41.corrections) | copy-start | bytes 393220 | tf_op jit(solution)/shard_map/cond
  2.0 18.5 %copy-start.9 = (s32[32]{0:T(128)S(1)}, s32[32]{0:T(128)}, u32[]{:S(2)}) copy-start(s32[32]{0:T(128)} %get-tuple-element.36.slots) | copy-start | bytes 388 | tf_op jit(solution)/shard_map/cond
  2.0 18.5 %copy-start.11 = (s32[16]{0:T(128)S(1)}, s32[16]{0:T(128)}, u32[]{:S(2)}) copy-start(s32[16]{0:T(128)} %get-tuple-element.37.ranks) | copy-start | bytes 196 | tf_op jit(solution)/shard_map/cond
  2.0 18.5 %copy-start = (f32[2,64,128,128]{3,2,1,0:T(8,128)S(1)}, f32[2,64,128,128]{3,2,1,0:T(8,128)}, u32[]{:S(2)}) copy-start(f32[2,64,128,128]{3,2,1,0:T(8,128)} %get-tuple-element.38.train) | copy-start | bytes 25165828 | tf_op jit(solution)/shard_map/cond
  5.3 23.2 %collective-permute-start.4 = (f32[4,16,8,128]{3,2,1,0:T(8,128)S(1)}, f32[4,16,8,128]{3,2,1,0:T(8,128)S(1)}, u32[]{:S(2)}, u32[]{:S(2)}) collective-permute-start(f32[4,16,8,128]{3,2,1,0:T(8,128)S(1)} %get-tuple-element.52), channel_id=1, source_target_pairs={{0,2},{1,3},{2,0},{3,1},{4,6},{5,7},{6,4},{7,5},{8,10},{9,11},{10,... | collective-permute-start | bytes 786440 | tf_op jit(solution)/shard_map/cond/branch_0_fun/ppermute | solution.py:245
  8.3 20.3 %collective-permute-start.6 = (f32[4,16,8,128]{3,2,1,0:T(8,128)S(1)}, f32[4,16,8,128]{3,2,1,0:T(8,128)S(1)}, u32[]{:S(2)}, u32[]{:S(2)}) collective-permute-start(f32[4,16,8,128]{3,2,1,0:T(8,128)S(1)} %get-tuple-element.53), channel_id=1, source_target_pairs={{0,12},{1,13},{2,14},{3,15},{4,8},{5,9},{6,10},{7,11},{8,4},{9,5},... | collective-permute-start | bytes 786440 | tf_op jit(solution)/shard_map/cond/branch_0_fun/ppermute | solution.py:245
  11.8 17.2 %collective-permute-start.10 = (f32[4,16,8,128]{3,2,1,0:T(8,128)S(1)}, f32[4,16,8,128]{3,2,1,0:T(8,128)S(1)}, u32[]{:S(2)}, u32[]{:S(2)}) collective-permute-start(f32[4,16,8,128]{3,2,1,0:T(8,128)S(1)} %get-tuple-element.55), channel_id=1, source_target_pairs={{0,6},{1,7},{2,4},{3,5},{4,2},{5,3},{6,0},{7,1},{8,14},{9,15},{10,... | collective-permute-start | bytes 786440 | tf_op jit(solution)/shard_map/cond/branch_0_fun/ppermute | solution.py:245
  11.8 22.2 %collective-permute-start.8 = (f32[4,16,8,128]{3,2,1,0:T(8,128)S(1)}, f32[4,16,8,128]{3,2,1,0:T(8,128)S(1)}, u32[]{:S(2)}, u32[]{:S(2)}) collective-permute-start(f32[4,16,8,128]{3,2,1,0:T(8,128)S(1)} %get-tuple-element.54), channel_id=1, source_target_pairs={{0,4},{1,5},{2,6},{3,7},{4,0},{5,1},{6,2},{7,3},{8,12},{9,13},{10,... | collective-permute-start | bytes 786440 | tf_op jit(solution)/shard_map/cond/branch_0_fun/ppermute | solution.py:245
  13.9 24.1 %collective-permute-start.12 = (f32[4,16,8,128]{3,2,1,0:T(8,128)S(1)}, f32[4,16,8,128]{3,2,1,0:T(8,128)S(1)}, u32[]{:S(2)}, u32[]{:S(2)}) collective-permute-start(f32[4,16,8,128]{3,2,1,0:T(8,128)S(1)} %get-tuple-element.56), channel_id=1, source_target_pairs={{0,14},{1,15},{2,12},{3,13},{4,10},{5,11},{6,8},{7,9},{8,6},{9,7},... | collective-permute-start | bytes 786440 | tf_op jit(solution)/shard_map/cond/branch_0_fun/ppermute | solution.py:245
  28.4 49.9 %collective-permute-start = (f32[2,8,8,16,128]{4,3,2,1,0:T(8,128)S(1)}, f32[2,8,8,16,128]{4,3,2,1,0:T(8,128)S(1)}, u32[]{:S(2)}, u32[]{:S(2)}) collective-permute-start(f32[2,8,8,16,128]{4,3,2,1,0:T(8,128)S(1)} %get-tuple-element.46), channel_id=1, source_target_pairs={{0,1},{1,0},{2,3},{3,2},{4,5},{5,4},{6,7},{7,6},{8,9},{9,8},{10,11... | collective-permute-start | bytes 3145736 | tf_op jit(solution)/shard_map/cond/branch_0_fun/ppermute | solution.py:258
  28.5 50.1 %collective-permute-start.1 = (f32[2,8,8,16,128]{4,3,2,1,0:T(8,128)S(1)}, f32[2,8,8,16,128]{4,3,2,1,0:T(8,128)S(1)}, u32[]{:S(2)}, u32[]{:S(2)}) collective-permute-start(f32[2,8,8,16,128]{4,3,2,1,0:T(8,128)S(1)} %get-tuple-element.47), channel_id=1, source_target_pairs={{0,1},{1,0},{2,3},{3,2},{4,5},{5,4},{6,7},{7,6},{8,9},{9,8},{10,11... | collective-permute-start | bytes 3145736 | tf_op jit(solution)/shard_map/cond/branch_0_fun/ppermute | solution.py:258
  29.0 51.3 %collective-permute-start.2 = (f32[2,8,8,16,128]{4,3,2,1,0:T(8,128)S(1)}, f32[2,8,8,16,128]{4,3,2,1,0:T(8,128)S(1)}, u32[]{:S(2)}, u32[]{:S(2)}) collective-permute-start(f32[2,8,8,16,128]{4,3,2,1,0:T(8,128)S(1)} %get-tuple-element.48), channel_id=1, source_target_pairs={{0,1},{1,0},{2,3},{3,2},{4,5},{5,4},{6,7},{7,6},{8,9},{9,8},{10,11... | collective-permute-start | bytes 3145736 | tf_op jit(solution)/shard_map/cond/branch_0_fun/ppermute | solution.py:258
  34.0 12.9 %collective-permute-start.14 = (f32[4,16,8,128]{3,2,1,0:T(8,128)S(1)}, f32[4,16,8,128]{3,2,1,0:T(8,128)S(1)}, u32[]{:S(2)}, u32[]{:S(2)}) collective-permute-start(f32[4,16,8,128]{3,2,1,0:T(8,128)S(1)} %get-tuple-element.57), channel_id=1, source_target_pairs={{0,8},{1,9},{2,10},{3,11},{4,12},{5,13},{6,14},{7,15},{8,0},{9,1},... | collective-permute-start | bytes 786440 | tf_op jit(solution)/shard_map/cond/branch_0_fun/ppermute | solution.py:245
  38.0 42.7 %collective-permute-start.3 = (f32[2,8,8,16,128]{4,3,2,1,0:T(8,128)S(1)}, f32[2,8,8,16,128]{4,3,2,1,0:T(8,128)S(1)}, u32[]{:S(2)}, u32[]{:S(2)}) collective-permute-start(f32[2,8,8,16,128]{4,3,2,1,0:T(8,128)S(1)} %get-tuple-element.49), channel_id=1, source_target_pairs={{0,1},{1,0},{2,3},{3,2},{4,5},{5,4},{6,7},{7,6},{8,9},{9,8},{10,11... | collective-permute-start | bytes 3145736 | tf_op jit(solution)/shard_map/cond/branch_0_fun/ppermute | solution.py:258
  46.9 14.8 %collective-permute-start.16 = (f32[4,16,8,128]{3,2,1,0:T(8,128)S(1)}, f32[4,16,8,128]{3,2,1,0:T(8,128)S(1)}, u32[]{:S(2)}, u32[]{:S(2)}) collective-permute-start(f32[4,16,8,128]{3,2,1,0:T(8,128)S(1)} %get-tuple-element.58), channel_id=1, source_target_pairs={{0,10},{1,11},{2,8},{3,9},{4,14},{5,15},{6,12},{7,13},{8,2},{9,3},... | collective-permute-start | bytes 786440 | tf_op jit(solution)/shard_map/cond/branch_0_fun/ppermute | solution.py:245
  61.8 7.9 %collective-permute-start.5 = (f32[4,16,8,128]{3,2,1,0:T(8,128)S(1)}, f32[4,16,8,128]{3,2,1,0:T(8,128)S(1)}, u32[]{:S(2)}, u32[]{:S(2)}) collective-permute-start(f32[4,16,8,128]{3,2,1,0:T(8,128)S(1)} %collective-permute-done.4.refs_9_), channel_id=1, source_target_pairs={{0,16},{16,0},{1,17},{17,1},{2,18},{18,2},{3,19},{19,3},{4,20},{20... | collective-permute-start | bytes 786440 | tf_op jit(solution)/shard_map/cond/branch_0_fun/ppermute | solution.py:251
  69.6 7.0 %collective-permute-start.7 = (f32[4,16,8,128]{3,2,1,0:T(8,128)S(1)}, f32[4,16,8,128]{3,2,1,0:T(8,128)S(1)}, u32[]{:S(2)}, u32[]{:S(2)}) collective-permute-start(f32[4,16,8,128]{3,2,1,0:T(8,128)S(1)} %collective-permute-done.6.refs_11_), channel_id=1, source_target_pairs={{0,16},{16,0},{1,17},{17,1},{2,18},{18,2},{3,19},{19,3},{4,20},{20... | collective-permute-start | bytes 786440 | tf_op jit(solution)/shard_map/cond/branch_0_fun/ppermute | solution.py:251
  76.6 9.2 %collective-permute-start.11 = (f32[4,16,8,128]{3,2,1,0:T(8,128)S(1)}, f32[4,16,8,128]{3,2,1,0:T(8,128)S(1)}, u32[]{:S(2)}, u32[]{:S(2)}) collective-permute-start(f32[4,16,8,128]{3,2,1,0:T(8,128)S(1)} %collective-permute-done.10.refs_11_), channel_id=1, source_target_pairs={{0,16},{16,0},{1,17},{17,1},{2,18},{18,2},{3,19},{19,3},{4,20},{20... | collective-permute-start | bytes 786440 | tf_op jit(solution)/shard_map/cond/branch_0_fun/ppermute | solution.py:251
  78.3 13.1 %collective-permute-start.9 = (f32[4,16,8,128]{3,2,1,0:T(8,128)S(1)}, f32[4,16,8,128]{3,2,1,0:T(8,128)S(1)}, u32[]{:S(2)}, u32[]{:S(2)}) collective-permute-start(f32[4,16,8,128]{3,2,1,0:T(8,128)S(1)} %collective-permute-done.8.refs_9_), channel_id=1, source_target_pairs={{0,16},{16,0},{1,17},{17,1},{2,18},{18,2},{3,19},{19,3},{4,20},{20... | collective-permute-start | bytes 786440 | tf_op jit(solution)/shard_map/cond/branch_0_fun/ppermute | solution.py:251
  78.6 18.4 %collective-permute-start.13 = (f32[4,16,8,128]{3,2,1,0:T(8,128)S(1)}, f32[4,16,8,128]{3,2,1,0:T(8,128)S(1)}, u32[]{:S(2)}, u32[]{:S(2)}) collective-permute-start(f32[4,16,8,128]{3,2,1,0:T(8,128)S(1)} %collective-permute-done.12.refs_9_), channel_id=1, source_target_pairs={{0,16},{16,0},{1,17},{17,1},{2,18},{18,2},{3,19},{19,3},{4,20},{20... | collective-permute-start | bytes 786440 | tf_op jit(solution)/shard_map/cond/branch_0_fun/ppermute | solution.py:251
  80.4 22.1 %collective-permute-start.15 = (f32[4,16,8,128]{3,2,1,0:T(8,128)S(1)}, f32[4,16,8,128]{3,2,1,0:T(8,128)S(1)}, u32[]{:S(2)}, u32[]{:S(2)}) collective-permute-start(f32[4,16,8,128]{3,2,1,0:T(8,128)S(1)} %collective-permute-done.14.refs_11_), channel_id=1, source_target_pairs={{0,16},{16,0},{1,17},{17,1},{2,18},{18,2},{3,19},{19,3},{4,20},{20... | collective-permute-start | bytes 786440 | tf_op jit(solution)/shard_map/cond/branch_0_fun/ppermute | solution.py:251
  80.7 24.6 %collective-permute-start.17 = (f32[4,16,8,128]{3,2,1,0:T(8,128)S(1)}, f32[4,16,8,128]{3,2,1,0:T(8,128)S(1)}, u32[]{:S(2)}, u32[]{:S(2)}) collective-permute-start(f32[4,16,8,128]{3,2,1,0:T(8,128)S(1)} %collective-permute-done.16.refs_9_), channel_id=1, source_target_pairs={{0,16},{16,0},{1,17},{17,1},{2,18},{18,2},{3,19},{19,3},{4,20},{20... | collective-permute-start | bytes 786440 | tf_op jit(solution)/shard_map/cond/branch_0_fun/ppermute | solution.py:251
  106.5 1.2 %collective-permute-start.18 = (f32[32,64]{1,0:T(8,128)S(1)}, f32[32,64]{1,0:T(8,128)S(1)}, u32[]{:S(2)}, u32[]{:S(2)}) collective-permute-start(f32[32,64]{1,0:T(8,128)S(1)} %score.14), channel_id=1, source_target_pairs={{0,1},{1,0},{2,3},{3,2},{4,5},{5,4},{6,7},{7,6},{8,9},{9,8},{10,11... | collective-permute-start | bytes 24584 | tf_op jit(solution)/shard_map/cond/branch_0_fun/ppermute | solution.py:268
  107.7 3.7 %collective-permute-start.19 = (f32[32,64]{1,0:T(8,128)S(1)}, f32[32,64]{1,0:T(8,128)S(1)}, u32[]{:S(2)}, u32[]{:S(2)}) collective-permute-start(f32[32,64]{1,0:T(8,128)S(1)} %add.29), channel_id=1, source_target_pairs={{0,2},{1,3},{2,0},{3,1},{4,6},{5,7},{6,4},{7,5},{8,10},{9,11},{10,... | collective-permute-start | bytes 24584 | tf_op jit(solution)/shard_map/cond/branch_0_fun/ppermute | solution.py:268
  107.7 3.8 %collective-permute-start.20 = (f32[32,64]{1,0:T(8,128)S(1)}, f32[32,64]{1,0:T(8,128)S(1)}, u32[]{:S(2)}, u32[]{:S(2)}) collective-permute-start(f32[32,64]{1,0:T(8,128)S(1)} %add.29), channel_id=1, source_target_pairs={{0,4},{1,5},{2,6},{3,7},{4,0},{5,1},{6,2},{7,3},{8,12},{9,13},{10,... | collective-permute-start | bytes 24584 | tf_op jit(solution)/shard_map/cond/branch_0_fun/ppermute | solution.py:268
  107.8 5.3 %collective-permute-start.21 = (f32[32,64]{1,0:T(8,128)S(1)}, f32[32,64]{1,0:T(8,128)S(1)}, u32[]{:S(2)}, u32[]{:S(2)}) collective-permute-start(f32[32,64]{1,0:T(8,128)S(1)} %add.29), channel_id=1, source_target_pairs={{0,6},{1,7},{2,4},{3,5},{4,2},{5,3},{6,0},{7,1},{8,14},{9,15},{10,... | collective-permute-start | bytes 24584 | tf_op jit(solution)/shard_map/cond/branch_0_fun/ppermute | solution.py:268
  113.1 4.6 %collective-permute-start.22 = (f32[32,64]{1,0:T(8,128)S(1)}, f32[32,64]{1,0:T(8,128)S(1)}, u32[]{:S(2)}, u32[]{:S(2)}) collective-permute-start(f32[32,64]{1,0:T(8,128)S(1)} %add_add_fusion), channel_id=1, source_target_pairs={{0,8},{1,9},{2,10},{3,11},{4,12},{5,13},{6,14},{7,15},{8,0},{9,1},... | collective-permute-start | bytes 24584 | tf_op jit(solution)/shard_map/cond/branch_0_fun/ppermute | solution.py:268
  117.7 0.6 copy-start.13
